TPU v7x, 768 devices: a whole 4x8x12 slice. The times are simulated.
768 devices in a mesh: dp: 48 (over z_lo, y, core), ctx: 4 (over z_hi), head: 4 (over x).
Axes of the slice: x: 4, y: 8, z: 12 (z_hi: 4, z_lo: 3; z = z_hi * 3 + z_lo), core: 2. Of those that a mesh axis runs over, the one named last changes fastest.
Arguments:
- query_long: bfloat16 [48, 512, 8192], P('dp', 'ctx', 'head'), may hold values from -6 to 6
- key_long: bfloat16 [48, 512, 1024], P('dp', 'ctx', 'head'), may hold values from -6 to 6
- long_values: bfloat16 [48, 512, 1024], P('dp', 'ctx', 'head'), may hold values from -6 to 6
- outgrad_long: bfloat16 [48, 512, 8192], P('dp', 'ctx', 'head'), may hold values from -6 to 6
- query_short: bfloat16 [48, 8, 64, 8192], P('dp', 'ctx', None, 'head'), may hold values from -6 to 6
- key_short: bfloat16 [48, 8, 64, 1024], P('dp', 'ctx', None, 'head'), may hold values from -6 to 6
- short_values: bfloat16 [48, 8, 64, 1024], P('dp', 'ctx', None, 'head'), may hold values from -6 to 6
- outgrad_short: bfloat16 [48, 8, 64, 8192], P('dp', 'ctx', None, 'head'), may hold values from -6 to 6
- segments: int32 [48, 8, 64], P('dp', 'ctx'), may hold values from 0 to 3, never falling along the last dimension, each value on 1 to 32 neighbouring positions
- assignment: int32 [48, 8], P('dp', 'ctx'), may hold values from 0 to 1, as said below
Outputs:
- output_long: bfloat16 [48, 512, 8192], P('dp', 'ctx', 'head')
- querygrad_long: bfloat16 [48, 512, 8192], P('dp', 'ctx', 'head')
- keygrad_long: bfloat16 [48, 512, 1024], P('dp', 'ctx', 'head')
- valuegrad_long: bfloat16 [48, 512, 1024], P('dp', 'ctx', 'head')
- output_short: bfloat16 [48, 8, 64, 8192], P('dp', 'ctx', None, 'head')
- querygrad_short: bfloat16 [48, 8, 64, 8192], P('dp', 'ctx', None, 'head')
- keygrad_short: bfloat16 [48, 8, 64, 1024], P('dp', 'ctx', None, 'head')
- valuegrad_short: bfloat16 [48, 8, 64, 1024], P('dp', 'ctx', None, 'head')
Inputs may be any that keep to these rules, and one draw needn't show every extreme that they name: In each group of 2 tiles of a sequence (tiles c * 2 to (c + 1) * 2 - 1) exactly 1 tiles have assignment 1. `segments`: segment numbers start at 0 in each tile and never fall along it.
All inputs are finite; a program needn't handle non-finite values.
Results may differ from a plain program's by a relative error of at most 0.02.
Values may be sent and summed in bfloat16 or wider, within the bound.
No kernel may reach another device: no remote copies, remote signals or barrier semaphores. Data moves between devices by JAX's collectives and lax.ppermute only.
A program may use at most 32 MiB of HBM per device.

v0:
```python
import math

import jax
import jax.numpy as jnp
from jax import lax
from jax.sharding import PartitionSpec as P

HEAD_SIZE = 128


def from_behind(value, axis, steps):
    count = lax.axis_size(axis)
    pairs = [(source, (source + steps) % count) for source in range(count)]
    return lax.ppermute(value, axis, pairs)


def attend(queries, key_rows, value_rows, out_grad, allowed):
    rows = queries.shape[0]
    cols = key_rows.shape[0]
    kv_heads = key_rows.shape[1] // HEAD_SIZE
    query_group = queries.shape[1] // key_rows.shape[1]
    scaling = 1.0 / math.sqrt(HEAD_SIZE)
    shaped_query = queries.reshape(rows, kv_heads, query_group, HEAD_SIZE)
    shaped_key = key_rows.reshape(cols, kv_heads, HEAD_SIZE)
    shaped_value = value_rows.reshape(cols, kv_heads, HEAD_SIZE)
    shaped_grad = out_grad.reshape(rows, kv_heads, query_group, HEAD_SIZE)
    scores = (
        jnp.einsum("rhgd,chd->hgrc", shaped_query, shaped_key, preferred_element_type=jnp.float32)
        * scaling
    )
    scores = jnp.where(allowed[None, None], scores, -jnp.inf)
    row_max = jnp.max(scores, axis=-1, keepdims=True)
    log_total = row_max + jnp.log(jnp.sum(jnp.exp(scores - row_max), axis=-1, keepdims=True))
    weights = jnp.exp(scores - log_total)
    weights_half = weights.astype(jnp.bfloat16)
    output = jnp.einsum(
        "hgrc,chd->rhgd", weights_half, shaped_value, preferred_element_type=jnp.float32
    ).astype(jnp.bfloat16)
    row_dots = jnp.sum(shaped_grad.astype(jnp.float32) * output.astype(jnp.float32), axis=-1)
    row_dots = jnp.transpose(row_dots, (1, 2, 0))[..., None]
    weight_grad = jnp.einsum(
        "rhgd,chd->hgrc", shaped_grad, shaped_value, preferred_element_type=jnp.float32
    )
    score_grad = (weights * (weight_grad - row_dots)).astype(jnp.bfloat16)
    querygrad = (
        jnp.einsum("hgrc,chd->rhgd", score_grad, shaped_key, preferred_element_type=jnp.float32)
        * scaling
    ).astype(jnp.bfloat16)
    keygrad = (
        jnp.einsum("hgrc,rhgd->chd", score_grad, shaped_query, preferred_element_type=jnp.float32)
        * scaling
    )
    valuegrad = jnp.einsum(
        "hgrc,rhgd->chd", weights_half, shaped_grad, preferred_element_type=jnp.float32
    )
    return (
        output.reshape(rows, -1),
        querygrad.reshape(rows, -1),
        keygrad.reshape(cols, -1),
        valuegrad.reshape(cols, -1),
    )


def tile_body(queries, key_rows, value_rows, out_grad, labels):
    position = lax.iota(jnp.int32, labels.shape[0])
    allowed = (labels[None, :] == labels[:, None]) & (position[None, :] <= position[:, None])
    output, querygrad, keygrad, valuegrad = attend(queries, key_rows, value_rows, out_grad, allowed)
    return (output, querygrad, keygrad.astype(jnp.bfloat16), valuegrad.astype(jnp.bfloat16))


def local(
    query_long,
    key_long,
    long_values,
    outgrad_long,
    query_short,
    key_short,
    short_values,
    outgrad_short,
    segments,
    assignment,
):
    gathered_keys, gathered_values = (
        lax.all_gather(key_long[0], "ctx", axis=0, tiled=True),
        lax.all_gather(long_values[0], "ctx", axis=0, tiled=True),
    )
    block_rows = query_long.shape[1]
    first_row = lax.axis_index("ctx") * block_rows
    query_pos = first_row + lax.iota(jnp.int32, block_rows)
    key_pos = lax.iota(jnp.int32, gathered_keys.shape[0])
    allowed = key_pos[None, :] <= query_pos[:, None]
    output, querygrad, key_part, value_part = attend(
        query_long[0], gathered_keys, gathered_values, outgrad_long[0], allowed
    )
    key_sum, value_sum = (
        lax.psum_scatter(
            key_part.astype(jnp.bfloat16).astype(jnp.float32).astype(jnp.bfloat16),
            "ctx",
            scatter_dimension=0,
            tiled=True,
        ).astype(jnp.float32),
        lax.psum_scatter(
            value_part.astype(jnp.bfloat16).astype(jnp.float32).astype(jnp.bfloat16),
            "ctx",
            scatter_dimension=0,
            tiled=True,
        ).astype(jnp.float32),
    )
    tile_count = query_short.shape[1]
    moving = tile_count // 2
    order = jnp.argsort(assignment[0], stable=True)
    kept = order[: tile_count - moving]
    sent = order[tile_count - moving :]
    short_inputs = (query_short[0], key_short[0], short_values[0], outgrad_short[0], segments[0])
    incoming = from_behind(
        (
            query_short[0][sent],
            key_short[0][sent],
            short_values[0][sent],
            outgrad_short[0][sent],
            segments[0][sent],
        ),
        "dp",
        1,
    )
    merged = [
        jnp.concatenate([member[kept], arriving], axis=0)
        for member, arriving in zip(short_inputs, incoming)
    ]
    short_results = jax.vmap(tile_body)(*merged)
    return (
        output[None],
        querygrad[None],
        key_sum.astype(jnp.bfloat16)[None],
        value_sum.astype(jnp.bfloat16)[None],
        short_results[0][None],
        short_results[1][None],
        short_results[2][None],
        short_results[3][None],
    )


def solution(mesh):
    in_specs = (
        P("dp", "ctx", "head"),
        P("dp", "ctx", "head"),
        P("dp", "ctx", "head"),
        P("dp", "ctx", "head"),
        P("dp", "ctx", None, "head"),
        P("dp", "ctx", None, "head"),
        P("dp", "ctx", None, "head"),
        P("dp", "ctx", None, "head"),
        P("dp", "ctx", None),
        P("dp", "ctx"),
    )
    out_specs = (
        P("dp", "ctx", "head"),
        P("dp", "ctx", "head"),
        P("dp", "ctx", "head"),
        P("dp", "ctx", "head"),
        P("dp", "ctx", None, "head"),
        P("dp", "ctx", None, "head"),
        P("dp", "ctx", None, "head"),
        P("dp", "ctx", None, "head"),
    )
    return jax.shard_map(local, mesh=mesh, in_specs=in_specs, out_specs=out_specs, check_vma=False)
```

profile of v0, /device:TPU:2, one launch (start us, length us, event | category | flops | bytes accessed | tf_op | source)
XLA Modules:
  0.0 142.6 jit_solution(13420585203777457706)
XLA Ops:
  7.2 1.3 copy.40
  8.5 25.9 %all-gather.1 = bf16[1,512,256]{2,1,0:T(8,128)(2,1)S(1)} all-gather(bf16[1,128,256]{2,1,0:T(8,128)(2,1)} %param.12), channel_id=3, replica_groups=mesh['dp'=48,'ctx'=4,'head'=4] {'ctx'}, dimensions={1}, use_global_device_ids=true | all-gather | bytes 327680 | tf_op jit(solution)/shard_map/all_gather | solution.py:85
  34.6 1.0 copy.35
  35.6 18.7 %all-gather = bf16[1,512,256]{1,2,0:T(8,128)(2,1)S(1)} all-gather(bf16[1,128,256]{1,2,0:T(8,128)(2,1)S(1)} %copy.35), channel_id=2, replica_groups=mesh['dp'=48,'ctx'=4,'head'=4] {'ctx'}, dimensions={1}, use_global_device_ids=true | all-gather | bytes 327680 | tf_op jit(solution)/shard_map/all_gather | solution.py:84
  54.4 1.3 copy.103
  57.4 2.0 %multiply_reduce_fusion.1 = (f32[128,2,8]{0,2,1:T(8,128)S(1)}, bf16[2,8,128,128]{2,3,1,0:T(8,128)(2,1)}) fusion(bf16[128,2,8,128]{0,3,2,1:T(8,128)(2,1)S(1)} %bitcast.173, bf16[512,2,128,1]{0,2,3,1:T(8,128)(2,1)S(1)} %bitcast.177, f32[2,512,128,8]{2,1,3,0:T(8,128)S(1)} %get-tuple-element.149, f32[2,8,128]{2,1,0:T(8,128)S(1)} %log_add_fusion.1, ...), kind=kOutput, calls=%fused_computation.38 | convolution fusion | flops 273938432 | bytes 5586944 | tf_op jit(solution)/shard_map/hgrc,chd->rhgd/dot_general | solution.py:36
  59.4 2.4 %fusion.1 = bf16[2,8,128,512]{2,3,1,0:T(8,128)(2,1)S(1)} fusion(f32[2,512,128,8]{2,1,3,0:T(8,128)S(1)} %get-tuple-element.149, bf16[512,2,128,1]{0,2,3,1:T(8,128)(2,1)} %bitcast.178, bf16[128,2,8,128]{0,3,2,1:T(8,128)(2,1)S(1)} %bitcast.174, f32[2,8,128]{2,1,0:T(8,128)S(1)} %bitcast.184, f32[2,8,128]{2,1,0:T(8,128)S(1)} %log_add_fusion.1, ...), kind=kOutput, calls=%fused_computation.2 | convolution fusion | flops 274726912 | bytes 7159808 | tf_op jit(solution)/shard_map/rhgd,chd->hgrc/dot_general | solution.py:41
  68.6 1.8 %dynamic-slice_bitcast_fusion.1 = (bf16[1,64,2048]{2,1,0:T(8,128)(2,1)S(1)}, bf16[1,64,2048]{2,1,0:T(8,128)(2,1)}) fusion(bf16[1,2,64,2048]{3,2,1,0:T(8,128)(2,1)} %param.17, s32[]{:T(128)} %bitcast.27, s32[]{:T(128)} %bitcast.29), kind=kLoop, calls=%fused_computation.47 | loop fusion | bytes 1048584 | tf_op jit(solution)/shard_map/gather | solution.py:127
  70.4 1.9 %collective-permute-start.4 = (bf16[1,64,2048]{2,1,0:T(8,128)(2,1)}, bf16[1,64,2048]{2,1,0:T(8,128)(2,1)}, u32[]{:S(2)}, u32[]{:S(2)}) collective-permute-start(bf16[1,64,2048]{2,1,0:T(8,128)(2,1)} %get-tuple-element.137), channel_id=1, source_target_pairs={{0,16},{16,32},{32,48},{48,64},{64,80},{80,96},{96,112},{112,128},... | collective-permute-start | bytes 786440 | tf_op jit(solution)/shard_map/ppermute | solution.py:14
  72.3 1.8 %dynamic-slice_bitcast_fusion.3 = (bf16[1,64,2048]{2,1,0:T(8,128)(2,1)S(1)}, bf16[1,64,2048]{2,1,0:T(8,128)(2,1)}) fusion(bf16[1,2,64,2048]{3,2,1,0:T(8,128)(2,1)} %param.14, s32[]{:T(128)} %bitcast.27, s32[]{:T(128)} %bitcast.29), kind=kLoop, calls=%fused_computation.49 | loop fusion | bytes 1048584 | tf_op jit(solution)/shard_map/gather | solution.py:127
  74.1 3.6 %collective-permute-start.3 = (bf16[1,64,2048]{2,1,0:T(8,128)(2,1)}, bf16[1,64,2048]{2,1,0:T(8,128)(2,1)}, u32[]{:S(2)}, u32[]{:S(2)}) collective-permute-start(bf16[1,64,2048]{2,1,0:T(8,128)(2,1)} %get-tuple-element.139), channel_id=1, source_target_pairs={{0,16},{16,32},{32,48},{48,64},{64,80},{80,96},{96,112},{112,128},... | collective-permute-start | bytes 786440 | tf_op jit(solution)/shard_map/ppermute | solution.py:14
  78.3 1.9 %collective-permute-start.2 = (bf16[1,64,256]{2,1,0:T(8,128)(2,1)}, bf16[1,64,256]{2,1,0:T(8,128)(2,1)}, u32[]{:S(2)}, u32[]{:S(2)}) collective-permute-start(bf16[1,64,256]{2,1,0:T(8,128)(2,1)} %get-tuple-element.143), channel_id=1, source_target_pairs={{0,16},{16,32},{32,48},{48,64},{64,80},{80,96},{96,112},{112,128},... | collective-permute-start | bytes 98312 | tf_op jit(solution)/shard_map/ppermute | solution.py:14
  80.9 3.6 %collective-permute-start.1 = (s32[1,64]{1,0:T(1,128)}, s32[1,64]{1,0:T(1,128)S(1)}, u32[]{:S(2)}, u32[]{:S(2)}) collective-permute-start(s32[1,64]{1,0:T(1,128)} %get-tuple-element.145), channel_id=1, source_target_pairs={{0,16},{16,32},{32,48},{48,64},{64,80},{80,96},{96,112},{112,128},... | collective-permute-start | bytes 776 | tf_op jit(solution)/shard_map/ppermute | solution.py:14
  85.1 2.1 %collective-permute-start = (bf16[1,64,256]{2,1,0:T(8,128)(2,1)}, bf16[1,64,256]{2,1,0:T(8,128)(2,1)}, u32[]{:S(2)}, u32[]{:S(2)}) collective-permute-start(bf16[1,64,256]{2,1,0:T(8,128)(2,1)} %get-tuple-element.141), channel_id=1, source_target_pairs={{0,16},{16,32},{32,48},{48,64},{64,80},{80,96},{96,112},{112,128},... | collective-permute-start | bytes 98312 | tf_op jit(solution)/shard_map/ppermute | solution.py:14
  87.2 3.4 %fusion.14 = bf16[2,512,128]{1,2,0:T(8,128)(2,1)S(1)} fusion(bf16[128,2,8,128]{0,3,2,1:T(8,128)(2,1)} %bitcast.175, f32[2,512,128,8]{2,1,3,0:T(8,128)} %copy-done, f32[2,8,128]{2,1,0:T(8,128)S(1)} %log_add_fusion.1, pred[128,512]{0,1:T(8,128)(4,1)S(1)} %iota_compare_fusion), kind=kOutput, calls=%fused_computation.26 | convolution fusion | flops 272760832 | bytes 5054464 | tf_op jit(solution)/shard_map/hgrc,rhgd->chd/dot_general | solution.py:53
  92.0 2.0 %copy.64 = bf16[1,128,2048]{2,1,0:T(8,128)(2,1)} copy(bf16[1,128,2048]{1,2,0:T(8,128)(2,1)} %bitcast.176) | data formatting | bytes 1048576
  94.0 1.0 copy.65
  96.7 1.0 pad_maximum_fusion.1
  97.9 1.0 pad_maximum_fusion
  101.3 1.1 fusion.12
  103.4 1.0 reshape.132
  104.4 1.4 copy.59
  105.8 1.0 reshape.134
  109.0 26.8 %reduce-scatter.5.cloned.1.call-done = bf16[128,256]{1,0:T(8,128)(2,1)} async-done(((bf16[512,256]{1,0:T(8,128)(2,1)}), bf16[128,256]{1,0:T(8,128)(2,1)}) %reduce-scatter.5.cloned.1.call-update) | async-done | bytes 65552 | tf_op jit(solution)/shard_map/reduce_scatter | solution.py:102
  (64 shorter events, 15.2 us)
Async XLA Ops:
  7.2 101.8 %reduce-scatter.3.cloned.1.call-start = ((), (), s32[]{:S(2)}) async-start(), calls=%async_computation.2 | async-start | bytes 327680 | tf_op jit(solution)/shard_map/reduce_scatter | solution.py:96
  8.5 50.8 %copy-start.1 = (bf16[1,128,2048]{1,2,0:T(8,128)(2,1)}, bf16[1,128,2048]{1,2,0:T(8,128)(2,1)S(1)}, u32[]{:S(2)}) copy-start(bf16[1,128,2048]{1,2,0:T(8,128)(2,1)S(1)} %copy.40) | copy-start | bytes 1572868
  34.6 22.8 %copy-start.2 = (bf16[1,512,256]{1,2,0:T(8,128)(2,1)}, bf16[1,512,256]{1,2,0:T(8,128)(2,1)S(1)}, u32[]{:S(2)}) copy-start(bf16[1,512,256]{1,2,0:T(8,128)(2,1)S(1)} %copy.38) | copy-start | bytes 786436
  56.5 2.9 %copy-start = (f32[2,512,128,8]{2,1,3,0:T(8,128)}, f32[2,512,128,8]{2,1,3,0:T(8,128)S(1)}, u32[]{:S(2)}) copy-start(f32[2,512,128,8]{2,1,3,0:T(8,128)S(1)} %get-tuple-element.149) | copy-start | bytes 12582916
  59.4 4.2 %copy-start.6 = (s32[1,2]{1,0:T(1,128)S(1)}, s32[1,2]{1,0:T(1,128)}, u32[]{:S(2)}) copy-start(s32[1,2]{1,0:T(1,128)} %param.19) | copy-start | bytes 28
  61.8 15.9 %copy-start.3 = (bf16[1,2,64,256]{3,2,1,0:T(8,128)(2,1)S(1)}, bf16[1,2,64,256]{3,2,1,0:T(8,128)(2,1)}, u32[]{:S(2)}) copy-start(bf16[1,2,64,256]{3,2,1,0:T(8,128)(2,1)} %param.15) | copy-start | bytes 196612
  61.8 18.5 %copy-start.5 = (s32[1,2,64]{2,1,0:T(2,128)S(1)}, s32[1,2,64]{2,1,0:T(2,128)}, u32[]{:S(2)}) copy-start(s32[1,2,64]{2,1,0:T(2,128)} %param.18) | copy-start | bytes 1540
  61.8 22.6 %copy-start.4 = (bf16[1,2,64,256]{3,2,1,0:T(8,128)(2,1)S(1)}, bf16[1,2,64,256]{3,2,1,0:T(8,128)(2,1)}, u32[]{:S(2)}) copy-start(bf16[1,2,64,256]{3,2,1,0:T(8,128)(2,1)} %param.16) | copy-start | bytes 196612
  63.5 72.2 %reduce-scatter.5.cloned.1.call-start = ((), (), s32[]{:S(2)}) async-start(), calls=%async_computation.3 | async-start | bytes 327680 | tf_op jit(solution)/shard_map/reduce_scatter | solution.py:102
  70.4 26.3 %collective-permute-start.4 = (bf16[1,64,2048]{2,1,0:T(8,128)(2,1)}, bf16[1,64,2048]{2,1,0:T(8,128)(2,1)}, u32[]{:S(2)}, u32[]{:S(2)}) collective-permute-start(bf16[1,64,2048]{2,1,0:T(8,128)(2,1)} %get-tuple-element.137), channel_id=1, source_target_pairs={{0,16},{16,32},{32,48},{48,64},{64,80},{80,96},{96,112},{112,128},... | collective-permute-start | bytes 786440 | tf_op jit(solution)/shard_map/ppermute | solution.py:14
  74.1 23.7 %collective-permute-start.3 = (bf16[1,64,2048]{2,1,0:T(8,128)(2,1)}, bf16[1,64,2048]{2,1,0:T(8,128)(2,1)}, u32[]{:S(2)}, u32[]{:S(2)}) collective-permute-start(bf16[1,64,2048]{2,1,0:T(8,128)(2,1)} %get-tuple-element.139), channel_id=1, source_target_pairs={{0,16},{16,32},{32,48},{48,64},{64,80},{80,96},{96,112},{112,128},... | collective-permute-start | bytes 786440 | tf_op jit(solution)/shard_map/ppermute | solution.py:14
  78.3 16.8 %collective-permute-start.2 = (bf16[1,64,256]{2,1,0:T(8,128)(2,1)}, bf16[1,64,256]{2,1,0:T(8,128)(2,1)}, u32[]{:S(2)}, u32[]{:S(2)}) collective-permute-start(bf16[1,64,256]{2,1,0:T(8,128)(2,1)} %get-tuple-element.143), channel_id=1, source_target_pairs={{0,16},{16,32},{32,48},{48,64},{64,80},{80,96},{96,112},{112,128},... | collective-permute-start | bytes 98312 | tf_op jit(solution)/shard_map/ppermute | solution.py:14
  80.9 14.1 %collective-permute-start.1 = (s32[1,64]{1,0:T(1,128)}, s32[1,64]{1,0:T(1,128)S(1)}, u32[]{:S(2)}, u32[]{:S(2)}) collective-permute-start(s32[1,64]{1,0:T(1,128)} %get-tuple-element.145), channel_id=1, source_target_pairs={{0,16},{16,32},{32,48},{48,64},{64,80},{80,96},{96,112},{112,128},... | collective-permute-start | bytes 776 | tf_op jit(solution)/shard_map/ppermute | solution.py:14
  85.1 10.8 %collective-permute-start = (bf16[1,64,256]{2,1,0:T(8,128)(2,1)}, bf16[1,64,256]{2,1,0:T(8,128)(2,1)}, u32[]{:S(2)}, u32[]{:S(2)}) collective-permute-start(bf16[1,64,256]{2,1,0:T(8,128)(2,1)} %get-tuple-element.141), channel_id=1, source_target_pairs={{0,16},{16,32},{32,48},{48,64},{64,80},{80,96},{96,112},{112,128},... | collective-permute-start | bytes 98312 | tf_op jit(solution)/shard_map/ppermute | solution.py:14
Sparse Core Ops, SparseCore 0:
  63.6 35.8 reduce-scatter.2
  103.1 32.5 reduce-scatter.4
where the time goes:
time: 143 us
  blocking collectives  44.6 us (31%)
  waiting for transfers between devices  26.8 us (19%)
  local copies, waits for them, and re-layouts  20.7 us (14%)
  between operations  18.3 us (13%)
  matrix products  13.5 us (9%)
  starting transfers between devices  13.1 us (9%)
  other arithmetic  5.56 us (4%)
    reduce_scatter x1, waiting for transfers between devices, local(): lax.psum_scatter(value_part.astype(jnp.bfloat16).astype(jnp.float32).asty...  26.8 us
    all_gather x1, blocking collectives, local(): lax.all_gather(long_values[0], 'ctx', axis=0, tiled=True)  25.9 us
    all_gather x1, blocking collectives, local(): lax.all_gather(key_long[0], 'ctx', axis=0, tiled=True)  18.7 us
    ppermute x5, starting transfers between devices, from_behind(): return lax.ppermute(value, axis, pairs)  13.1 us
    unnamed x20, local copies, waits for them, and re-layouts  5.6 us
    gather x5, local copies, waits for them, and re-layouts, local(): member[kept]  5.43 us
    dot_general x2, matrix products, attend(): jnp.einsum('hgrc,rhgd->chd', weights_half, shaped_grad, preferred_element...  3.76 us
    concatenate x5, other arithmetic, local(): jnp.concatenate([member[kept], arriving], axis=0)  3.54 us
  transfers between devices with their start and end apart: 7, of which 1 were waited for; matrix products, arithmetic and copies ran while one was open for 20% of the time, Pallas kernels for 0%

commit v1 on v0

v1 whole, which is shorter than its diff:
```python
import math

import jax
import jax.numpy as jnp
from jax import lax
from jax.experimental import pallas as pl
from jax.experimental.pallas import tpu as pltpu
from jax.sharding import PartitionSpec as P

HEAD = 128
SCALE = 1.0 / math.sqrt(HEAD)
EXP2_SCALE = SCALE / math.log(2.0)
MASKED = -1e30
F32 = jnp.float32
BF16 = jnp.bfloat16


def dot_nt(a, b):
    return lax.dot_general(a, b, (((1,), (1,)), ((), ())), preferred_element_type=F32)


def dot_nn(a, b):
    return jnp.dot(a, b, preferred_element_type=F32)


def dot_tn(a, b):
    return lax.dot_general(a, b, (((0,), (0,)), ((), ())), preferred_element_type=F32)


def attend(q, g, k, v, bias):
    raw = dot_nt(q, k) + bias
    top = jnp.max(raw, axis=-1, keepdims=True)
    grown = jnp.exp2((raw - top) * EXP2_SCALE)
    weights = grown * (1.0 / jnp.sum(grown, axis=-1, keepdims=True))
    half = weights.astype(BF16)
    out = dot_nn(half, v).astype(BF16)
    weight_grad = dot_nt(g, v)
    row_dots = jnp.sum(g.astype(F32) * out.astype(F32), axis=-1, keepdims=True)
    score_grad = (weights * (weight_grad - row_dots)).astype(BF16)
    q_grad = (dot_nn(score_grad, k) * SCALE).astype(BF16)
    return half, score_grad, out, q_grad


def heads_of(ref, first, count, rows):
    return jnp.concatenate(
        [ref[rows, (first + j) * HEAD:(first + j + 1) * HEAD] for j in range(count)], axis=0
    )


def pack_kv(k_ref, v_ref, o_ref):
    o_ref[:, :256] = k_ref[...]
    o_ref[:, 256:] = v_ref[...]


def pack_tile(where_ref, q_ref, g_ref, k_ref, v_ref, seg_ref, o_ref):
    at = 1 - where_ref[0, 0]
    o_ref[:, 0:2048] = q_ref[0]
    o_ref[:, 2048:4096] = g_ref[0]
    o_ref[:, 4096:4352] = k_ref[0]
    o_ref[:, 4352:4608] = v_ref[0]
    labels = seg_ref[pl.ds(at, 1), :].astype(F32)
    plane = jnp.concatenate([labels, jnp.zeros_like(labels)], axis=1)
    o_ref[:, 4608:4736] = jnp.broadcast_to(plane, (64, 128)).astype(BF16)


def long_kernel(q_ref, g_ref, own_k, own_v, one_ref, two_ref, three_ref,
                out_ref, qg_ref, own_o, one_o, two_o, three_o, *, group):
    place = lax.axis_index("ctx")
    rows = q_ref.shape[0]
    shape = (rows, 4 * rows)
    col = lax.broadcasted_iota(jnp.int32, shape, 1)
    row = lax.broadcasted_iota(jnp.int32, shape, 0)
    allowed = ((col < rows) & (col <= row)) | ((col >= rows) & (col < (place + 1) * rows))
    bias = jnp.where(allowed, 0.0, MASKED).astype(F32)
    bias = jnp.concatenate([bias] * group, axis=0)
    for h in range(2):
        ks = slice(h * HEAD, (h + 1) * HEAD)
        vs = slice(256 + h * HEAD, 256 + (h + 1) * HEAD)
        k = jnp.concatenate([own_k[:, ks], one_ref[:, ks], two_ref[:, ks], three_ref[:, ks]], axis=0)
        v = jnp.concatenate([own_v[:, ks], one_ref[:, vs], two_ref[:, vs], three_ref[:, vs]], axis=0)
        k_sum = jnp.zeros((HEAD, 4 * rows), F32)
        v_sum = jnp.zeros((HEAD, 4 * rows), F32)
        for first in range(h * 8, h * 8 + 8, group):
            q = heads_of(q_ref, first, group, slice(None))
            g = heads_of(g_ref, first, group, slice(None))
            half, score_grad, out, q_grad = attend(q, g, k, v, bias)
            for j in range(group):
                at = slice((first + j) * HEAD, (first + j + 1) * HEAD)
                out_ref[:, at] = out[j * rows:(j + 1) * rows]
                qg_ref[:, at] = q_grad[j * rows:(j + 1) * rows]
            k_sum = k_sum + dot_tn(q, score_grad)
            v_sum = v_sum + dot_tn(g, half)
        k_grad = jnp.transpose(k_sum * SCALE).astype(BF16)
        v_grad = jnp.transpose(v_sum).astype(BF16)
        for i, ref in enumerate((own_o, one_o, two_o, three_o)):
            ref[:, ks] = k_grad[i * rows:(i + 1) * rows]
            ref[:, vs] = v_grad[i * rows:(i + 1) * rows]


def tile_work(q_ref, g_ref, k_ref, v_ref, labels, store):
    rows = 64
    seen = lax.broadcasted_iota(jnp.int32, (8, rows), 0).astype(F32)
    onehot = (seen == jnp.broadcast_to(labels, (8, rows))).astype(F32)
    same = dot_tn(onehot, onehot)
    col = lax.broadcasted_iota(jnp.int32, (rows, rows), 1)
    row = lax.broadcasted_iota(jnp.int32, (rows, rows), 0)
    bias = jnp.where((same > 0.5) & (col <= row), 0.0, MASKED).astype(F32)
    bias = jnp.concatenate([bias] * 8, axis=0)
    for h in range(2):
        ks = slice(h * HEAD, (h + 1) * HEAD)
        k, v = k_ref[:, ks], v_ref[:, ks]
        q = heads_of(q_ref, h * 8, 8, slice(None))
        g = heads_of(g_ref, h * 8, 8, slice(None))
        half, score_grad, out, q_grad = attend(q, g, k, v, bias)
        k_grad = (dot_tn(score_grad, q) * SCALE).astype(BF16)
        v_grad = dot_tn(half, g).astype(BF16)
        store(h, out, q_grad, k_grad, v_grad)


def store_tile(out_ref, qg_ref, kg_ref, vg_ref, h, out, q_grad, k_grad, v_grad):
    for j in range(8):
        at = slice((h * 8 + j) * HEAD, (h * 8 + j + 1) * HEAD)
        out_ref[0, :, at] = out[j * 64:(j + 1) * 64]
        qg_ref[0, :, at] = q_grad[j * 64:(j + 1) * 64]
    ks = slice(h * HEAD, (h + 1) * HEAD)
    kg_ref[0, :, ks] = k_grad
    vg_ref[0, :, ks] = v_grad


def kept_kernel(where_ref, q_ref, g_ref, k_ref, v_ref, seg_ref, out_ref, qg_ref, kg_ref, vg_ref):
    labels = seg_ref[pl.ds(where_ref[0, 0], 1), :].astype(F32)

    def store(*results):
        store_tile(out_ref, qg_ref, kg_ref, vg_ref, *results)

    tile_work(q_ref.at[0], g_ref.at[0], k_ref.at[0], v_ref.at[0], labels, store)


def moved_kernel(pack_ref, a, b, c, d, out_ref, qg_ref, kg_ref, vg_ref):
    labels = pack_ref[0:1, 4608:4672].astype(F32)

    def store(*results):
        store_tile(out_ref, qg_ref, kg_ref, vg_ref, *results)

    tile_work(
        pack_ref.at[:, 0:2048], pack_ref.at[:, 2048:4096], pack_ref.at[:, 4096:4352],
        pack_ref.at[:, 4352:4608], labels, store,
    )


def finish(own, one, two, three, k_ref, v_ref):
    total = own[...].astype(F32) + one[...].astype(F32) + two[...].astype(F32) + three[...].astype(F32)
    k_ref[...] = total[:, :256].astype(BF16)
    v_ref[...] = total[:, 256:].astype(BF16)


def shaped(*shape):
    return jax.ShapeDtypeStruct(shape, BF16)


def cost(flops, moved, exps):
    return pl.CostEstimate(flops=flops, bytes_accessed=moved, transcendentals=exps)


def send(value, axis, pairs):
    return lax.ppermute(value, axis, pairs)


def local(query_long, key_long, long_values, outgrad_long, query_short, key_short,
          short_values, outgrad_short, segments, assignment):
    kv = pl.pallas_call(
        pack_kv, out_shape=shaped(128, 512), name="pack_kv",
        cost_estimate=cost(0, 1 << 18, 0),
    )(key_long[0], long_values[0])
    size = lax.axis_size("ctx")
    behind = [
        send(kv, "ctx", [(c, c + step) for c in range(size - step)]) for step in (1, 2, 3)
    ]

    short = (query_short[0], outgrad_short[0], key_short[0], short_values[0])
    widths = (2048, 2048, 256, 256)
    seg_spec = pl.BlockSpec((2, 64), lambda i, where: (0, 0))
    pack = pl.pallas_call(
        pack_tile,
        grid_spec=pltpu.PrefetchScalarGridSpec(
            num_scalar_prefetch=1, grid=(1,),
            in_specs=[pl.BlockSpec((1, 64, w), lambda i, where: (1 - where[0, 0], 0, 0)) for w in widths]
            + [seg_spec],
            out_specs=pl.BlockSpec((64, 4736), lambda i, where: (0, 0)),
        ),
        out_shape=shaped(64, 4736), name="pack_tile",
        cost_estimate=cost(0, 1 << 20, 0),
    )(assignment, *short, segments[0])
    count = lax.axis_size("dp")
    arrived = send(pack, "dp", [(c, (c + 1) % count) for c in range(count)])

    tile_cost = cost(2 * 6 * 16 * 64 * 64 * 128, 1 << 20, 16 * 64 * 64)
    tile_shapes = [shaped(2, 64, w) for w in widths]
    kept = pl.pallas_call(
        kept_kernel,
        grid_spec=pltpu.PrefetchScalarGridSpec(
            num_scalar_prefetch=1, grid=(1,),
            in_specs=[pl.BlockSpec((1, 64, w), lambda i, where: (where[0, 0], 0, 0)) for w in widths]
            + [seg_spec],
            out_specs=[pl.BlockSpec((1, 64, w), lambda i, where: (0, 0, 0)) for w in widths],
        ),
        out_shape=tile_shapes, name="kept_tile",
        cost_estimate=tile_cost,
    )(assignment, *short, segments[0])

    rows = query_long.shape[1]
    results = pl.pallas_call(
        lambda *refs: long_kernel(*refs, group=2),
        out_shape=[shaped(rows, 2048), shaped(rows, 2048)] + [shaped(rows, 512)] * 4,
        name="long_block",
        cost_estimate=cost(2 * 6 * 16 * 128 * 512 * 128, 3 << 20, 16 * 128 * 512),
    )(query_long[0], outgrad_long[0], key_long[0], long_values[0], *behind)
    output, querygrad, own = results[:3]
    parts = [
        send(part, "ctx", [(c, c - step) for c in range(step, size)])
        for step, part in zip((1, 2, 3), results[3:])
    ]

    tiles = pl.pallas_call(
        moved_kernel,
        grid=(1,),
        in_specs=[pl.BlockSpec((64, 4736), lambda i: (0, 0))]
        + [pl.BlockSpec(memory_space=pl.ANY)] * 4,
        out_specs=[pl.BlockSpec((1, 64, w), lambda i: (1, 0, 0)) for w in widths],
        out_shape=tile_shapes, name="moved_tile",
        input_output_aliases={1: 0, 2: 1, 3: 2, 4: 3},
        cost_estimate=tile_cost,
    )(arrived, *kept)

    key_sum, value_sum = pl.pallas_call(
        finish, out_shape=[shaped(rows, 256)] * 2, name="finish",
        cost_estimate=cost(1 << 18, 1 << 19, 0),
    )(own, *parts)
    return (
        output[None], querygrad[None], key_sum[None], value_sum[None],
        tiles[0][None], tiles[1][None], tiles[2][None], tiles[3][None],
    )


def solution(mesh):
    long_spec = P("dp", "ctx", "head")
    tile_spec = P("dp", "ctx", None, "head")
    return jax.shard_map(
        local, mesh=mesh,
        in_specs=(long_spec,) * 4 + (tile_spec,) * 4 + (P("dp", "ctx", None), P("dp", "ctx")),
        out_specs=(long_spec,) * 4 + (tile_spec,) * 4,
        check_vma=False,
    )
```

time: 143 us -> 82.6 us (0.58)
  the two profiles are of different devices: /device:TPU:2 before, /device:TPU:147 now
where the time goes in v1:
time: 82.6 us; the launch traced here: 82.1 us
  waiting for transfers between devices  31 us (38%)
  starting transfers between devices  26.9 us (33%)
  Pallas kernels  21.4 us (26%)
  local copies, waits for them, and re-layouts  2.14 us (3%)
    ppermute x7, waiting for transfers between devices, send(): return lax.ppermute(value, axis, pairs)  31 us
    ppermute x7, starting transfers between devices, send(): return lax.ppermute(value, axis, pairs)  26.9 us
    pallas_call x1, Pallas kernels, local(): pl.pallas_call(lambda *refs: long_kernel(*refs, group=2), out_shape=[shap...  8.29 us
    pallas_call x1, Pallas kernels, local(): pl.pallas_call(kept_kernel, grid_spec=pltpu.PrefetchScalarGridSpec(num_sc...  3.91 us
    pallas_call x1, Pallas kernels, local(): pl.pallas_call(moved_kernel, grid=(1,), in_specs=[pl.BlockSpec((64, 4736)...  3.25 us
    pallas_call x1, Pallas kernels, local(): pl.pallas_call(pack_tile, grid_spec=pltpu.PrefetchScalarGridSpec(num_scal...  2.6 us
    unnamed x14, local copies, waits for them, and re-layouts  2.14 us
    pallas_call x1, Pallas kernels, local(): pl.pallas_call(finish, out_shape=[shaped(rows, 256)] * 2, name='finish',...  1.79 us
  transfers between devices with their start and end apart: 7, of which 5 were waited for; matrix products, arithmetic and copies ran while one was open for 0% of the time, Pallas kernels for 19%

profile of v1, /device:TPU:147, one launch (start us, length us, event | category | flops | bytes accessed | tf_op | source)
XLA Modules:
  0.0 82.1 jit_solution(3466975370884826038)
XLA Ops:
  0.6 2.6 %pack_tile.1 = bf16[64,4736]{1,0:T(8,128)(2,1)} custom-call(s32[1,2]{1,0:T(1,128)} %where_ref.3, bf16[2,64,2048]{2,1,0:T(8,128)(2,1)} %bitcast.17, bf16[2,64,2048]{2,1,0:T(8,128)(2,1)} %bitcast.19, bf16[2,64,256]{2,1,0:T(8,128)(2,1)} %bitcast.23, bf16[2,64,256]{2,1,0:T(8,128)(2,1)} %bitcast.25, s32[2,64]{1,0:T(2,128)} %bitcast.33), custom_call_target="tpu_custom_call" | custom-call | bytes 1048576 | tf_op jit(solution)/shard_map/pack_tile/pallas_call | solution.py:183
  3.2 3.8 %collective-permute-start.6 = (bf16[64,4736]{1,0:T(8,128)(2,1)}, bf16[64,4736]{1,0:T(8,128)(2,1)S(1)}, u32[]{:S(2)}, u32[]{:S(2)}) collective-permute-start(bf16[64,4736]{1,0:T(8,128)(2,1)} %pack_tile.1), channel_id=1, source_target_pairs={{0,16},{16,32},{32,48},{48,64},{64,80},{80,96},{96,112},{112,128},... | collective-permute-start | bytes 1818632 | tf_op jit(solution)/shard_map/ppermute | solution.py:166
  7.0 1.5 %pack_kv.1 = bf16[128,512]{1,0:T(8,128)(2,1)} custom-call(bf16[128,256]{1,0:T(8,128)(2,1)} %bitcast.29, bf16[128,256]{1,0:T(8,128)(2,1)} %bitcast.31), custom_call_target="tpu_custom_call" | custom-call | bytes 262144 | tf_op jit(solution)/shard_map/pack_kv/pallas_call | solution.py:171
  8.5 12.5 %collective-permute-start.2 = (bf16[128,512]{1,0:T(8,128)(2,1)}, bf16[128,512]{1,0:T(8,128)(2,1)S(1)}, u32[]{:S(2)}, u32[]{:S(2)}) collective-permute-start(bf16[128,512]{1,0:T(8,128)(2,1)} %pack_kv.1), channel_id=1, source_target_pairs={{0,12},{1,13},{2,14},{3,15},{16,28},{17,29},{18,30},{19,31},{32,44... | collective-permute-start | bytes 393224 | tf_op jit(solution)/shard_map/ppermute | solution.py:166
  21.0 1.3 %collective-permute-start.1 = (bf16[128,512]{1,0:T(8,128)(2,1)}, bf16[128,512]{1,0:T(8,128)(2,1)S(1)}, u32[]{:S(2)}, u32[]{:S(2)}) collective-permute-start(bf16[128,512]{1,0:T(8,128)(2,1)} %pack_kv.1), channel_id=1, source_target_pairs={{0,8},{4,12},{1,9},{5,13},{2,10},{6,14},{3,11},{7,15},{16,24},{20,... | collective-permute-start | bytes 393224 | tf_op jit(solution)/shard_map/ppermute | solution.py:166
  22.3 5.5 %collective-permute-start = (bf16[128,512]{1,0:T(8,128)(2,1)}, bf16[128,512]{1,0:T(8,128)(2,1)S(1)}, u32[]{:S(2)}, u32[]{:S(2)}) collective-permute-start(bf16[128,512]{1,0:T(8,128)(2,1)} %pack_kv.1), channel_id=1, source_target_pairs={{0,4},{4,8},{8,12},{1,5},{5,9},{9,13},{2,6},{6,10},{10,14},{3,7},{... | collective-permute-start | bytes 393224 | tf_op jit(solution)/shard_map/ppermute | solution.py:166
  27.8 0.0 collective-permute-done.2.refs_6_
  27.8 0.0 copy-start.4
  27.8 0.3 collective-permute-done.1.refs_5_
  28.1 8.5 %collective-permute-done.refs_4_ = bf16[128,512]{1,0:T(8,128)(2,1)S(1)} collective-permute-done((bf16[128,512]{1,0:T(8,128)(2,1)}, bf16[128,512]{1,0:T(8,128)(2,1)S(1)}, u32[]{:S(2)}, u32[]{:S(2)}) %collective-permute-start) | collective-permute-done | bytes 131104 | tf_op jit(solution)/shard_map/ppermute | solution.py:166
  36.6 0.6 copy-done.6
  37.3 8.3 %long_block.1 = (bf16[128,2048]{1,0:T(8,128)(2,1)}, bf16[128,2048]{1,0:T(8,128)(2,1)}, bf16[128,512]{1,0:T(8,128)(2,1)}, bf16[128,512]{1,0:T(8,128)(2,1)}, bf16[...) custom-call(bf16[128,2048]{1,0:T(8,128)(2,1)} %bitcast.35, bf16[128,2048]{1,0:T(8,128)(2,1)} %bitcast.36, ...), custom_call_target="tpu_custom_call" | custom-call | flops 1610612736 | bytes 3145728 | tf_op jit(solution)/shard_map/long_block/pallas_call | solution.py:212
  45.6 1.3 %collective-permute-start.3 = (bf16[128,512]{1,0:T(8,128)(2,1)}, bf16[128,512]{1,0:T(8,128)(2,1)S(1)}, u32[]{:S(2)}, u32[]{:S(2)}) collective-permute-start(bf16[128,512]{1,0:T(8,128)(2,1)} %get-tuple-element.27), channel_id=1, source_target_pairs={{4,0},{8,4},{12,8},{5,1},{9,5},{13,9},{6,2},{10,6},{14,10},{7,3},{... | collective-permute-start | bytes 393224 | tf_op jit(solution)/shard_map/ppermute | solution.py:166
  46.9 1.3 %collective-permute-start.4 = (bf16[128,512]{1,0:T(8,128)(2,1)}, bf16[128,512]{1,0:T(8,128)(2,1)S(1)}, u32[]{:S(2)}, u32[]{:S(2)}) collective-permute-start(bf16[128,512]{1,0:T(8,128)(2,1)} %get-tuple-element.28), channel_id=1, source_target_pairs={{8,0},{12,4},{9,1},{13,5},{10,2},{14,6},{11,3},{15,7},{24,16},{28,... | collective-permute-start | bytes 393224 | tf_op jit(solution)/shard_map/ppermute | solution.py:166
  48.2 1.3 %collective-permute-start.5 = (bf16[128,512]{1,0:T(8,128)(2,1)}, bf16[128,512]{1,0:T(8,128)(2,1)S(1)}, u32[]{:S(2)}, u32[]{:S(2)}) collective-permute-start(bf16[128,512]{1,0:T(8,128)(2,1)} %get-tuple-element.29), channel_id=1, source_target_pairs={{12,0},{13,1},{14,2},{15,3},{28,16},{29,17},{30,18},{31,19},{44,32... | collective-permute-start | bytes 393224 | tf_op jit(solution)/shard_map/ppermute | solution.py:166
  49.5 3.9 %kept_tile.1 = (bf16[2,64,2048]{2,1,0:T(8,128)(2,1)}, bf16[2,64,2048]{2,1,0:T(8,128)(2,1)}, bf16[2,64,256]{2,1,0:T(8,128)(2,1)}, bf16[2,64,256]{2,1,0:T(8,128)(2,1)}) custom-call(s32[1,2]{1,0:T(1,128)} %where_ref.3, bf16[2,64,2048]{2,1,0:T(8,128)(2,1)} %bitcast.18, bf16[2,64,2048]{2,1,0:T(8,128)(2,1)} %bitcast.20, bf16[2,64,256]{2,1,0:T(8,128)(2,1)} %bitcast.24, ...), custom_call_target="tpu_custom_call" | custom-call | flops 100663296 | bytes 1048576 | tf_op jit(solution)/shard_map/kept_tile/pallas_call | solution.py:199
  53.4 2.7 %collective-permute-done.3.one = bf16[128,512]{1,0:T(8,128)(2,1)S(1)} collective-permute-done((bf16[128,512]{1,0:T(8,128)(2,1)}, bf16[128,512]{1,0:T(8,128)(2,1)S(1)}, u32[]{:S(2)}, u32[]{:S(2)}) %collective-permute-start.3) | collective-permute-done | bytes 131104 | tf_op jit(solution)/shard_map/ppermute | solution.py:166
  56.1 7.8 %collective-permute-done.4.two = bf16[128,512]{1,0:T(8,128)(2,1)S(1)} collective-permute-done((bf16[128,512]{1,0:T(8,128)(2,1)}, bf16[128,512]{1,0:T(8,128)(2,1)S(1)}, u32[]{:S(2)}, u32[]{:S(2)}) %collective-permute-start.4) | collective-permute-done | bytes 131104 | tf_op jit(solution)/shard_map/ppermute | solution.py:166
  63.9 11.7 %collective-permute-done.5.three = bf16[128,512]{1,0:T(8,128)(2,1)S(1)} collective-permute-done((bf16[128,512]{1,0:T(8,128)(2,1)}, bf16[128,512]{1,0:T(8,128)(2,1)S(1)}, u32[]{:S(2)}, u32[]{:S(2)}) %collective-permute-start.5) | collective-permute-done | bytes 131104 | tf_op jit(solution)/shard_map/ppermute | solution.py:166
  75.6 0.6 copy-done.3
  76.2 1.8 %finish.1 = (bf16[128,256]{1,0:T(8,128)(2,1)}, bf16[128,256]{1,0:T(8,128)(2,1)}) custom-call(bf16[128,512]{1,0:T(8,128)(2,1)} %get-tuple-element.26.own, bf16[128,512]{1,0:T(8,128)(2,1)} %copy-done.1, bf16[128,512]{1,0:T(8,128)(2,1)} %copy-done.2, bf16[128,512]{1,0:T(8,128)(2,1)} %copy-done.3), custom_call_target="tpu_custom_call" | custom-call | flops 262144 | bytes 524288 | tf_op jit(solution)/shard_map/finish/pallas_call | solution.py:235
  78.0 0.0 collective-permute-done.6.pack_ref
  78.0 0.8 %copy-done = bf16[64,4736]{1,0:T(8,128)(2,1)} copy-done((bf16[64,4736]{1,0:T(8,128)(2,1)}, bf16[64,4736]{1,0:T(8,128)(2,1)S(1)}, u32[]{:S(2)}) %copy-start) | copy-done | bytes 606232
  78.9 3.3 %moved_tile.1 = (bf16[2,64,2048]{2,1,0:T(8,128)(2,1)}, bf16[2,64,2048]{2,1,0:T(8,128)(2,1)}, bf16[2,64,256]{2,1,0:T(8,128)(2,1)}, bf16[2,64,256]{2,1,0:T(8,128)(2,1)}) custom-call(bf16[64,4736]{1,0:T(8,128)(2,1)} %copy-done, bf16[2,64,2048]{2,1,0:T(8,128)(2,1)} %get-tuple-element.32.a, ...), custom_call_target="tpu_custom_call", output_to_operand_aliasing={{0}: (1, {}), {1}: (2, {}), {2}: (3, {}), {3}: (4, {})} | custom-call | flops 100663296 | bytes 1048576 | tf_op jit(solution)/shard_map/moved_tile/pallas_call | solution.py:224
  (10 shorter events, 0.0 us)
Async XLA Ops:
  3.2 74.8 %collective-permute-start.6 = (bf16[64,4736]{1,0:T(8,128)(2,1)}, bf16[64,4736]{1,0:T(8,128)(2,1)S(1)}, u32[]{:S(2)}, u32[]{:S(2)}) collective-permute-start(bf16[64,4736]{1,0:T(8,128)(2,1)} %pack_tile.1), channel_id=1, source_target_pairs={{0,16},{16,32},{32,48},{48,64},{64,80},{80,96},{96,112},{112,128},... | collective-permute-start | bytes 1818632 | tf_op jit(solution)/shard_map/ppermute | solution.py:166
  8.5 19.3 %collective-permute-start.2 = (bf16[128,512]{1,0:T(8,128)(2,1)}, bf16[128,512]{1,0:T(8,128)(2,1)S(1)}, u32[]{:S(2)}, u32[]{:S(2)}) collective-permute-start(bf16[128,512]{1,0:T(8,128)(2,1)} %pack_kv.1), channel_id=1, source_target_pairs={{0,12},{1,13},{2,14},{3,15},{16,28},{17,29},{18,30},{19,31},{32,44... | collective-permute-start | bytes 393224 | tf_op jit(solution)/shard_map/ppermute | solution.py:166
  21.0 7.1 %collective-permute-start.1 = (bf16[128,512]{1,0:T(8,128)(2,1)}, bf16[128,512]{1,0:T(8,128)(2,1)S(1)}, u32[]{:S(2)}, u32[]{:S(2)}) collective-permute-start(bf16[128,512]{1,0:T(8,128)(2,1)} %pack_kv.1), channel_id=1, source_target_pairs={{0,8},{4,12},{1,9},{5,13},{2,10},{6,14},{3,11},{7,15},{16,24},{20,... | collective-permute-start | bytes 393224 | tf_op jit(solution)/shard_map/ppermute | solution.py:166
  22.3 14.3 %collective-permute-start = (bf16[128,512]{1,0:T(8,128)(2,1)}, bf16[128,512]{1,0:T(8,128)(2,1)S(1)}, u32[]{:S(2)}, u32[]{:S(2)}) collective-permute-start(bf16[128,512]{1,0:T(8,128)(2,1)} %pack_kv.1), channel_id=1, source_target_pairs={{0,4},{4,8},{8,12},{1,5},{5,9},{9,13},{2,6},{6,10},{10,14},{3,7},{... | collective-permute-start | bytes 393224 | tf_op jit(solution)/shard_map/ppermute | solution.py:166
  27.8 8.8 %copy-start.4 = (bf16[128,512]{1,0:T(8,128)(2,1)}, bf16[128,512]{1,0:T(8,128)(2,1)S(1)}, u32[]{:S(2)}) copy-start(bf16[128,512]{1,0:T(8,128)(2,1)S(1)} %collective-permute-done.2.refs_6_) | copy-start | bytes 393220
  28.1 8.5 %copy-start.5 = (bf16[128,512]{1,0:T(8,128)(2,1)}, bf16[128,512]{1,0:T(8,128)(2,1)S(1)}, u32[]{:S(2)}) copy-start(bf16[128,512]{1,0:T(8,128)(2,1)S(1)} %collective-permute-done.1.refs_5_) | copy-start | bytes 393220
  36.6 0.7 copy-start.6
  45.6 10.5 %collective-permute-start.3 = (bf16[128,512]{1,0:T(8,128)(2,1)}, bf16[128,512]{1,0:T(8,128)(2,1)S(1)}, u32[]{:S(2)}, u32[]{:S(2)}) collective-permute-start(bf16[128,512]{1,0:T(8,128)(2,1)} %get-tuple-element.27), channel_id=1, source_target_pairs={{4,0},{8,4},{12,8},{5,1},{9,5},{13,9},{6,2},{10,6},{14,10},{7,3},{... | collective-permute-start | bytes 393224 | tf_op jit(solution)/shard_map/ppermute | solution.py:166
  46.9 17.0 %collective-permute-start.4 = (bf16[128,512]{1,0:T(8,128)(2,1)}, bf16[128,512]{1,0:T(8,128)(2,1)S(1)}, u32[]{:S(2)}, u32[]{:S(2)}) collective-permute-start(bf16[128,512]{1,0:T(8,128)(2,1)} %get-tuple-element.28), channel_id=1, source_target_pairs={{8,0},{12,4},{9,1},{13,5},{10,2},{14,6},{11,3},{15,7},{24,16},{28,... | collective-permute-start | bytes 393224 | tf_op jit(solution)/shard_map/ppermute | solution.py:166
  48.2 27.4 %collective-permute-start.5 = (bf16[128,512]{1,0:T(8,128)(2,1)}, bf16[128,512]{1,0:T(8,128)(2,1)S(1)}, u32[]{:S(2)}, u32[]{:S(2)}) collective-permute-start(bf16[128,512]{1,0:T(8,128)(2,1)} %get-tuple-element.29), channel_id=1, source_target_pairs={{12,0},{13,1},{14,2},{15,3},{28,16},{29,17},{30,18},{31,19},{44,32... | collective-permute-start | bytes 393224 | tf_op jit(solution)/shard_map/ppermute | solution.py:166
  56.1 19.5 %copy-start.1 = (bf16[128,512]{1,0:T(8,128)(2,1)}, bf16[128,512]{1,0:T(8,128)(2,1)S(1)}, u32[]{:S(2)}) copy-start(bf16[128,512]{1,0:T(8,128)(2,1)S(1)} %collective-permute-done.3.one) | copy-start | bytes 393220
  63.9 11.7 %copy-start.2 = (bf16[128,512]{1,0:T(8,128)(2,1)}, bf16[128,512]{1,0:T(8,128)(2,1)S(1)}, u32[]{:S(2)}) copy-start(bf16[128,512]{1,0:T(8,128)(2,1)S(1)} %collective-permute-done.4.two) | copy-start | bytes 393220
  75.6 0.6 copy-start.3
  78.0 0.8 %copy-start = (bf16[64,4736]{1,0:T(8,128)(2,1)}, bf16[64,4736]{1,0:T(8,128)(2,1)S(1)}, u32[]{:S(2)}) copy-start(bf16[64,4736]{1,0:T(8,128)(2,1)S(1)} %collective-permute-done.6.pack_ref) | copy-start | bytes 1818628

commit v2 on v1

v2 whole, which is shorter than its diff:
```python
import math

import jax
import jax.numpy as jnp
from jax import lax
from jax.experimental import pallas as pl
from jax.experimental.pallas import tpu as pltpu
from jax.sharding import PartitionSpec as P


HEAD = 128
SCALE = 1.0 / math.sqrt(HEAD)
EXP2_SCALE = SCALE / math.log(2.0)
MASKED = -1e30
GROUP = 8
F32 = jnp.float32
BF16 = jnp.bfloat16


def dot_nt(a, b):
    return lax.dot_general(a, b, (((1,), (1,)), ((), ())), preferred_element_type=F32)


def dot_nn(a, b):
    return jnp.dot(a, b, preferred_element_type=F32)


def dot_tn(a, b):
    return lax.dot_general(a, b, (((0,), (0,)), ((), ())), preferred_element_type=F32)


def attend(q, g, k, v, bias):
    raw = dot_nt(q, k) + bias
    top = jnp.max(raw, axis=-1, keepdims=True)
    grown = jnp.exp2((raw - top) * EXP2_SCALE)
    weights = grown * (1.0 / jnp.sum(grown, axis=-1, keepdims=True))
    half = weights.astype(BF16)
    out = dot_nn(half, v).astype(BF16)
    weight_grad = dot_nt(g, v)
    row_dots = jnp.sum(g.astype(F32) * out.astype(F32), axis=-1, keepdims=True)
    score_grad = (weights * (weight_grad - row_dots)).astype(BF16)
    q_grad = (dot_nn(score_grad, k) * SCALE).astype(BF16)
    return half, score_grad, out, q_grad


def heads_of(ref, first, count, rows):
    return jnp.concatenate(
        [ref[rows, (first + j) * HEAD:(first + j + 1) * HEAD] for j in range(count)], axis=0
    )


def pack_tile(where_ref, q_ref, g_ref, k_ref, v_ref, seg_ref, o_ref):
    at = 1 - where_ref[0, 0]
    o_ref[:, 0:2048] = q_ref[0]
    o_ref[:, 2048:4096] = g_ref[0]
    o_ref[:, 4096:4352] = k_ref[0]
    o_ref[:, 4352:4608] = v_ref[0]
    labels = seg_ref[pl.ds(at, 1), :].astype(F32)
    plane = jnp.concatenate([labels, jnp.zeros_like(labels)], axis=1)
    o_ref[:, 4608:4736] = jnp.broadcast_to(plane, (64, 128)).astype(BF16)


def long_head(q_ref, g_ref, own_ref, near_one, near_two, far_one, far_two, far_three, *rest, head, group):
    out_ref, qg_ref, own_o, one_o, two_o, three_o = rest[-6:]
    place = lax.axis_index("ctx")
    rows = q_ref.shape[0]
    shape = (rows, 4 * rows)
    col = lax.broadcasted_iota(jnp.int32, shape, 1)
    row = lax.broadcasted_iota(jnp.int32, shape, 0)
    allowed = ((col < rows) & (col <= row)) | ((col >= rows) & (col < (place + 1) * rows))
    bias = jnp.where(allowed, 0.0, MASKED).astype(F32)
    bias = jnp.concatenate([bias] * group, axis=0)

    def keys_of(first):
        at = slice(first + head * HEAD, first + (head + 1) * HEAD)
        return jnp.concatenate([
            own_ref[:, at], near_one[:, at] + far_one[:, at], near_two[:, at] + far_two[:, at], far_three[:, at],
        ], axis=0)

    k, v = keys_of(0), keys_of(2 * HEAD)
    k_sum = jnp.zeros((HEAD, 4 * rows), F32)
    v_sum = jnp.zeros((HEAD, 4 * rows), F32)
    for first in range(0, 8, group):
        q = heads_of(q_ref, first, group, slice(None))
        g = heads_of(g_ref, first, group, slice(None))
        half, score_grad, out, q_grad = attend(q, g, k, v, bias)
        for j in range(group):
            at = slice((first + j) * HEAD, (first + j + 1) * HEAD)
            out_ref[:, at] = out[j * rows:(j + 1) * rows]
            qg_ref[:, at] = q_grad[j * rows:(j + 1) * rows]
        k_sum = k_sum + dot_tn(q, score_grad)
        v_sum = v_sum + dot_tn(g, half)
    k_grad = jnp.transpose(k_sum * SCALE).astype(BF16)
    v_grad = jnp.transpose(v_sum).astype(BF16)
    for i, ref in enumerate((own_o, one_o, two_o, three_o)):
        ref[:, :HEAD] = k_grad[i * rows:(i + 1) * rows]
        ref[:, HEAD:] = v_grad[i * rows:(i + 1) * rows]


def tile_work(q_ref, g_ref, k_ref, v_ref, labels, store):
    rows = 64
    seen = lax.broadcasted_iota(jnp.int32, (8, rows), 0).astype(F32)
    onehot = (seen == jnp.broadcast_to(labels, (8, rows))).astype(F32)
    same = dot_tn(onehot, onehot)
    col = lax.broadcasted_iota(jnp.int32, (rows, rows), 1)
    row = lax.broadcasted_iota(jnp.int32, (rows, rows), 0)
    bias = jnp.where((same > 0.5) & (col <= row), 0.0, MASKED).astype(F32)
    bias = jnp.concatenate([bias] * 8, axis=0)
    for h in range(2):
        ks = slice(h * HEAD, (h + 1) * HEAD)
        k, v = k_ref[:, ks], v_ref[:, ks]
        q = heads_of(q_ref, h * 8, 8, slice(None))
        g = heads_of(g_ref, h * 8, 8, slice(None))
        half, score_grad, out, q_grad = attend(q, g, k, v, bias)
        k_grad = (dot_tn(score_grad, q) * SCALE).astype(BF16)
        v_grad = dot_tn(half, g).astype(BF16)
        store(h, out, q_grad, k_grad, v_grad)


def store_tile(out_ref, qg_ref, kg_ref, vg_ref, h, out, q_grad, k_grad, v_grad):
    for j in range(8):
        at = slice((h * 8 + j) * HEAD, (h * 8 + j + 1) * HEAD)
        out_ref[0, :, at] = out[j * 64:(j + 1) * 64]
        qg_ref[0, :, at] = q_grad[j * 64:(j + 1) * 64]
    ks = slice(h * HEAD, (h + 1) * HEAD)
    kg_ref[0, :, ks] = k_grad
    vg_ref[0, :, ks] = v_grad


def kept_kernel(where_ref, q_ref, g_ref, k_ref, v_ref, seg_ref, out_ref, qg_ref, kg_ref, vg_ref):
    labels = seg_ref[pl.ds(where_ref[0, 0], 1), :].astype(F32)

    def store(*results):
        store_tile(out_ref, qg_ref, kg_ref, vg_ref, *results)

    tile_work(q_ref.at[0], g_ref.at[0], k_ref.at[0], v_ref.at[0], labels, store)


def moved_kernel(early_ref, late_ref, a, b, c, d, out_ref, qg_ref, kg_ref, vg_ref, pack_ref):
    pack_ref[...] = early_ref[...] + late_ref[...]
    labels = pack_ref[0:1, 4608:4672].astype(F32)

    def store(*results):
        store_tile(out_ref, qg_ref, kg_ref, vg_ref, *results)

    tile_work(
        pack_ref.at[:, 0:2048], pack_ref.at[:, 2048:4096], pack_ref.at[:, 4096:4352],
        pack_ref.at[:, 4352:4608], labels, store,
    )


def finish(*refs):
    k_ref, v_ref = refs[-2:]
    for h in range(2):
        total = sum(ref[...].astype(F32) for ref in refs[4 * h:4 * h + 4])
        at = slice(h * HEAD, (h + 1) * HEAD)
        k_ref[:, at] = total[:, :HEAD].astype(BF16)
        v_ref[:, at] = total[:, HEAD:].astype(BF16)


def shaped(*shape):
    return jax.ShapeDtypeStruct(shape, BF16)


def cost(flops, moved, exps):
    return pl.CostEstimate(flops=flops, bytes_accessed=moved, transcendentals=exps)


def grant(mib):
    return pltpu.CompilerParams(vmem_limit_bytes=mib << 20)


def work(query_long, key_long, long_values, outgrad_long, query_short, key_short,
         short_values, outgrad_short, segments, assignment):
    rows = query_long.shape[1]
    size = lax.axis_size("ctx")
    whole = pl.BlockSpec(memory_space=pltpu.VMEM)
    packed = jnp.concatenate([key_long[0], long_values[0]], axis=1)
    last = size - 1
    near = [lax.ppermute(packed, "ctx", [(c, c + step) for c in range(last - step)]) for step in (1, 2)]
    far = [lax.ppermute(packed, "ctx", [(last - step, last)]) for step in (1, 2, 3)]

    short = (query_short[0], outgrad_short[0], key_short[0], short_values[0])
    widths = (2048, 2048, 256, 256)
    seg_spec = pl.BlockSpec((2, 64), lambda i, where: (0, 0))
    pack = pl.pallas_call(
        pack_tile,
        grid_spec=pltpu.PrefetchScalarGridSpec(
            num_scalar_prefetch=1, grid=(1,),
            in_specs=[pl.BlockSpec((1, 64, w), lambda i, where: (1 - where[0, 0], 0, 0)) for w in widths]
            + [seg_spec],
            out_specs=pl.BlockSpec((64, 4736), lambda i, where: (0, 0)),
        ),
        out_shape=shaped(64, 4736), name="pack_tile",
        cost_estimate=cost(0, 1 << 20, 0), compiler_params=grant(6),
    )(assignment, *short, segments[0])
    count = lax.axis_size("dp")
    pairs = [
        (source * size + c, (source + 1) % count * size + c) for source in range(count) for c in range(size)
    ]
    late = [((count - 1) * size, 0)]
    early = [pair for pair in pairs if pair not in late]
    arrived = lax.ppermute(pack, ("dp", "ctx"), early)
    arrived_late = lax.ppermute(pack, ("dp", "ctx"), late)

    tile_cost = cost(2 * 6 * 16 * 64 * 64 * 128, 1 << 20, 16 * 64 * 64)
    tile_shapes = [shaped(2, 64, w) for w in widths]
    kept = pl.pallas_call(
        kept_kernel,
        grid_spec=pltpu.PrefetchScalarGridSpec(
            num_scalar_prefetch=1, grid=(1,),
            in_specs=[pl.BlockSpec((1, 64, w), lambda i, where: (where[0, 0], 0, 0)) for w in widths]
            + [seg_spec],
            out_specs=[pl.BlockSpec((1, 64, w), lambda i, where: (0, 0, 0)) for w in widths],
        ),
        out_shape=tile_shapes, name="kept_tile",
        cost_estimate=tile_cost, compiler_params=grant(16),
    )(assignment, *short, segments[0])

    wide = [shaped(rows, 2048), shaped(rows, 2048)]
    done = []
    parts = []
    for h in range(2):
        half_spec = pl.BlockSpec((rows, 1024), lambda i, h=h: (0, h))
        results = pl.pallas_call(
            lambda *refs, h=h: long_head(*refs, head=h, group=GROUP),
            grid=(1,),
            in_specs=[half_spec, half_spec] + [whole] * 6
            + [pl.BlockSpec(memory_space=pl.ANY)] * len(done),
            out_specs=[half_spec, half_spec] + [whole] * 4,
            out_shape=wide + [shaped(rows, 256)] * 4,
            input_output_aliases={8: 0, 9: 1} if done else {},
            cost_estimate=cost(6 * 8 * 128 * 512 * 128, 3 << 19, 8 * 128 * 512),
            compiler_params=grant(24),
        )(query_long[0], outgrad_long[0], packed, *near, *far, *done)
        done = results[:2]
        parts += [results[2]] + [
            lax.ppermute(part, "ctx", [(c, c - step) for c in range(step, size)])
            for step, part in zip((1, 2, 3), results[3:])
        ]

    tiles = pl.pallas_call(
        moved_kernel,
        grid=(1,),
        in_specs=[whole] * 2
        + [pl.BlockSpec(memory_space=pl.ANY)] * 4,
        out_specs=[pl.BlockSpec((1, 64, w), lambda i: (1, 0, 0)) for w in widths],
        out_shape=tile_shapes, name="moved_tile",
        input_output_aliases={2: 0, 3: 1, 4: 2, 5: 3},
        scratch_shapes=[pltpu.VMEM((64, 4736), BF16)],
        cost_estimate=tile_cost, compiler_params=grant(16),
    )(arrived, arrived_late, *kept)

    key_sum, value_sum = pl.pallas_call(
        finish, out_shape=[shaped(rows, 256)] * 2, name="finish",
        cost_estimate=cost(1 << 18, 1 << 19, 0), compiler_params=grant(4),
    )(*parts)
    return (
        done[0][None], done[1][None], key_sum[None], value_sum[None],
        tiles[0][None], tiles[1][None], tiles[2][None], tiles[3][None],
    )


def solution(mesh):
    long_spec = P("dp", "ctx", "head")
    tile_spec = P("dp", "ctx", None, "head")
    return jax.shard_map(
        work, mesh=mesh,
        in_specs=(long_spec,) * 4 + (tile_spec,) * 4 + (P("dp", "ctx", None), P("dp", "ctx")),
        out_specs=(long_spec,) * 4 + (tile_spec,) * 4,
        check_vma=False,
    )
```

time: 82.6 us -> 85.4 us (1.034)
  the two profiles are of different devices: /device:TPU:147 before, /device:TPU:77 now
where the time goes in v2:
time: 85.4 us; the launch traced here: 84.8 us
  waiting for transfers between devices  38.7 us (45%)
  starting transfers between devices  29.5 us (35%)
  Pallas kernels  11.3 us (13%)
  local copies, waits for them, and re-layouts  4.46 us (5%)
  between operations  0.86 us (1%)
    ppermute x6, waiting for transfers between devices, work(): lax.ppermute(part, 'ctx', [(c, c - step) for c in range(step, size)])  20.2 us
    ppermute x3, starting transfers between devices, work(): lax.ppermute(packed, 'ctx', [(last - step, last)])  14.7 us
    ppermute x3, waiting for transfers between devices, work(): lax.ppermute(packed, 'ctx', [(last - step, last)])  9.7 us
    ppermute x2, waiting for transfers between devices, work(): lax.ppermute(packed, 'ctx', [(c, c + step) for c in range(last - step)])  8.79 us
    ppermute x6, starting transfers between devices, work(): lax.ppermute(part, 'ctx', [(c, c - step) for c in range(step, size)])  7.72 us
    pallas_call x2, Pallas kernels, work(): pl.pallas_call(lambda *refs, h=h: long_head(*refs, head=h, group=GROUP),...  5.08 us
    unnamed x28, local copies, waits for them, and re-layouts  4.46 us
    ppermute x1, starting transfers between devices, work(): arrived = lax.ppermute(pack, ('dp', 'ctx'), early)  3.77 us
  transfers between devices with their start and end apart: 13, of which 7 were waited for; matrix products, arithmetic and copies ran while one was open for 0% of the time, Pallas kernels for 10%

profile of v2, /device:TPU:77, one launch (start us, length us, event | category | flops | bytes accessed | tf_op | source)
XLA Modules:
  0.0 84.8 jit_solution(17469622226620307499)
XLA Ops:
  1.3 1.0 %copy-done = bf16[1,2,64,2048]{3,2,1,0:T(8,128)(2,1)S(1)} copy-done((bf16[1,2,64,2048]{3,2,1,0:T(8,128)(2,1)S(1)}, bf16[1,2,64,2048]{3,2,1,0:T(8,128)(2,1)}, u32[]{:S(2)}) %copy-start) | copy-done | bytes 524312
  2.4 1.0 %copy-done.2 = bf16[1,2,64,2048]{3,2,1,0:T(8,128)(2,1)S(1)} copy-done((bf16[1,2,64,2048]{3,2,1,0:T(8,128)(2,1)S(1)}, bf16[1,2,64,2048]{3,2,1,0:T(8,128)(2,1)}, u32[]{:S(2)}) %copy-start.2) | copy-done | bytes 524312
  3.4 0.8 copy-done.6
  4.2 0.8 copy-done.8
  6.4 3.8 %collective-permute-start.11 = (bf16[64,4736]{1,0:T(8,128)(2,1)S(1)}, bf16[64,4736]{1,0:T(8,128)(2,1)S(1)}, u32[]{:S(2)}, u32[]{:S(2)}) collective-permute-start(bf16[64,4736]{1,0:T(8,128)(2,1)S(1)} %pack_tile.1), channel_id=1, source_target_pairs={{0,16},{4,20},{8,24},{12,28},{16,32},{20,36},{24,40},{28,44},{32,4... | collective-permute-start | bytes 1818632 | tf_op jit(solution)/shard_map/ppermute | solution.py:203
  10.2 13.4 %collective-permute-start.4 = (bf16[128,512]{1,0:T(8,128)(2,1)S(1)}, bf16[128,512]{1,0:T(8,128)(2,1)S(1)}, u32[]{:S(2)}, u32[]{:S(2)}) collective-permute-start(bf16[128,512]{1,0:T(8,128)(2,1)S(1)} %pad_maximum_fusion.refs_2_), channel_id=1, source_target_pairs={{0,12},{1,13},{2,14},{3,15},{16,28},{17,29},{18,30},{19,31},{32,44... | collective-permute-start | bytes 393224 | tf_op jit(solution)/shard_map/ppermute | solution.py:181
  25.0 9.7 %collective-permute-done.4.refs_7_ = bf16[128,512]{1,0:T(8,128)(2,1)S(1)} collective-permute-done((bf16[128,512]{1,0:T(8,128)(2,1)S(1)}, bf16[128,512]{1,0:T(8,128)(2,1)S(1)}, u32[]{:S(2)}, u32[]{:S(2)}) %collective-permute-start.4) | collective-permute-done | bytes 131104 | tf_op jit(solution)/shard_map/ppermute | solution.py:181
  34.7 1.3 %collective-permute-start.1 = (bf16[128,512]{1,0:T(8,128)(2,1)S(1)}, bf16[128,512]{1,0:T(8,128)(2,1)S(1)}, u32[]{:S(2)}, u32[]{:S(2)}) collective-permute-start(bf16[128,512]{1,0:T(8,128)(2,1)S(1)} %pad_maximum_fusion.refs_2_), channel_id=1, source_target_pairs={{0,8},{1,9},{2,10},{3,11},{16,24},{17,25},{18,26},{19,27},{32,40},... | collective-permute-start | bytes 393224 | tf_op jit(solution)/shard_map/ppermute | solution.py:180
  36.0 1.3 %collective-permute-start = (bf16[128,512]{1,0:T(8,128)(2,1)S(1)}, bf16[128,512]{1,0:T(8,128)(2,1)S(1)}, u32[]{:S(2)}, u32[]{:S(2)}) collective-permute-start(bf16[128,512]{1,0:T(8,128)(2,1)S(1)} %pad_maximum_fusion.refs_2_), channel_id=1, source_target_pairs={{0,4},{4,8},{1,5},{5,9},{2,6},{6,10},{3,7},{7,11},{16,20},{20,24},... | collective-permute-start | bytes 393224 | tf_op jit(solution)/shard_map/ppermute | solution.py:180
  37.3 1.9 %collective-permute-done.1.refs_4_ = bf16[128,512]{1,0:T(8,128)(2,1)S(1)} collective-permute-done((bf16[128,512]{1,0:T(8,128)(2,1)S(1)}, bf16[128,512]{1,0:T(8,128)(2,1)S(1)}, u32[]{:S(2)}, u32[]{:S(2)}) %collective-permute-start.1) | collective-permute-done | bytes 131104 | tf_op jit(solution)/shard_map/ppermute | solution.py:180
  39.2 6.9 %collective-permute-done.refs_3_ = bf16[128,512]{1,0:T(8,128)(2,1)S(1)} collective-permute-done((bf16[128,512]{1,0:T(8,128)(2,1)S(1)}, bf16[128,512]{1,0:T(8,128)(2,1)S(1)}, u32[]{:S(2)}, u32[]{:S(2)}) %collective-permute-start) | collective-permute-done | bytes 131104 | tf_op jit(solution)/shard_map/ppermute | solution.py:180
  46.1 2.5 %shard_map.161 = (bf16[128,2048]{1,0:T(8,128)(2,1)}, bf16[128,2048]{1,0:T(8,128)(2,1)}, bf16[128,256]{1,0:T(8,128)(2,1)S(1)}, bf16[128,256]{1,0:T(8,128)(2,1)S(1...) custom-call(bf16[128,2048]{1,0:T(8,128)(2,1)S(1)} %bitcast.21, bf16[128,2048]{1,0:T(8,128)(2,1)S(1)} %bitcast.23, ...), custom_call_target="tpu_custom_call" | custom-call | flops 402653184 | bytes 1572864 | tf_op jit(solution)/shard_map/pallas_call | solution.py:225
  48.6 2.5 %shard_map.162 = (bf16[128,2048]{1,0:T(8,128)(2,1)}, bf16[128,2048]{1,0:T(8,128)(2,1)}, bf16[128,256]{1,0:T(8,128)(2,1)S(1)}, bf16[128,256]{1,0:T(8,128)(2,1)S(1...) custom-call(bf16[128,2048]{1,0:T(8,128)(2,1)S(1)} %bitcast.22, ...), custom_call_target="tpu_custom_call", output_to_operand_aliasing={{0}: (8, {}), {1}: (9, {})} | custom-call | flops 402653184 | bytes 1572864 | tf_op jit(solution)/shard_map/pallas_call | solution.py:225
  51.2 1.3 %collective-permute-start.8 = (bf16[128,256]{1,0:T(8,128)(2,1)S(1)}, bf16[128,256]{1,0:T(8,128)(2,1)S(1)}, u32[]{:S(2)}, u32[]{:S(2)}) collective-permute-start(bf16[128,256]{1,0:T(8,128)(2,1)S(1)} %get-tuple-element.39), channel_id=1, source_target_pairs={{4,0},{8,4},{12,8},{5,1},{9,5},{13,9},{6,2},{10,6},{14,10},{7,3},{... | collective-permute-start | bytes 196616 | tf_op jit(solution)/shard_map/ppermute | solution.py:238
  52.5 1.3 %collective-permute-start.9 = (bf16[128,256]{1,0:T(8,128)(2,1)S(1)}, bf16[128,256]{1,0:T(8,128)(2,1)S(1)}, u32[]{:S(2)}, u32[]{:S(2)}) collective-permute-start(bf16[128,256]{1,0:T(8,128)(2,1)S(1)} %get-tuple-element.40), channel_id=1, source_target_pairs={{8,0},{12,4},{9,1},{13,5},{10,2},{14,6},{11,3},{15,7},{24,16},{28,... | collective-permute-start | bytes 196616 | tf_op jit(solution)/shard_map/ppermute | solution.py:238
  53.8 1.3 %collective-permute-start.10 = (bf16[128,256]{1,0:T(8,128)(2,1)S(1)}, bf16[128,256]{1,0:T(8,128)(2,1)S(1)}, u32[]{:S(2)}, u32[]{:S(2)}) collective-permute-start(bf16[128,256]{1,0:T(8,128)(2,1)S(1)} %get-tuple-element.41), channel_id=1, source_target_pairs={{12,0},{13,1},{14,2},{15,3},{28,16},{29,17},{30,18},{31,19},{44,32... | collective-permute-start | bytes 196616 | tf_op jit(solution)/shard_map/ppermute | solution.py:238
  55.1 8.1 %collective-permute-done.8.refs_5_ = bf16[128,256]{1,0:T(8,128)(2,1)S(1)} collective-permute-done((bf16[128,256]{1,0:T(8,128)(2,1)S(1)}, bf16[128,256]{1,0:T(8,128)(2,1)S(1)}, u32[]{:S(2)}, u32[]{:S(2)}) %collective-permute-start.8) | collective-permute-done | bytes 65568 | tf_op jit(solution)/shard_map/ppermute | solution.py:238
  63.1 1.3 %collective-permute-start.5 = (bf16[128,256]{1,0:T(8,128)(2,1)S(1)}, bf16[128,256]{1,0:T(8,128)(2,1)S(1)}, u32[]{:S(2)}, u32[]{:S(2)}) collective-permute-start(bf16[128,256]{1,0:T(8,128)(2,1)S(1)} %get-tuple-element.35), channel_id=1, source_target_pairs={{4,0},{8,4},{12,8},{5,1},{9,5},{13,9},{6,2},{10,6},{14,10},{7,3},{... | collective-permute-start | bytes 196616 | tf_op jit(solution)/shard_map/ppermute | solution.py:238
  64.4 4.7 %collective-permute-done.9.refs_6_ = bf16[128,256]{1,0:T(8,128)(2,1)S(1)} collective-permute-done((bf16[128,256]{1,0:T(8,128)(2,1)S(1)}, bf16[128,256]{1,0:T(8,128)(2,1)S(1)}, u32[]{:S(2)}, u32[]{:S(2)}) %collective-permute-start.9) | collective-permute-done | bytes 65568 | tf_op jit(solution)/shard_map/ppermute | solution.py:238
  69.2 1.3 %collective-permute-start.6 = (bf16[128,256]{1,0:T(8,128)(2,1)S(1)}, bf16[128,256]{1,0:T(8,128)(2,1)S(1)}, u32[]{:S(2)}, u32[]{:S(2)}) collective-permute-start(bf16[128,256]{1,0:T(8,128)(2,1)S(1)} %get-tuple-element.36), channel_id=1, source_target_pairs={{8,0},{12,4},{9,1},{13,5},{10,2},{14,6},{11,3},{15,7},{24,16},{28,... | collective-permute-start | bytes 196616 | tf_op jit(solution)/shard_map/ppermute | solution.py:238
  70.5 1.3 %collective-permute-start.7 = (bf16[128,256]{1,0:T(8,128)(2,1)S(1)}, bf16[128,256]{1,0:T(8,128)(2,1)S(1)}, u32[]{:S(2)}, u32[]{:S(2)}) collective-permute-start(bf16[128,256]{1,0:T(8,128)(2,1)S(1)} %get-tuple-element.37), channel_id=1, source_target_pairs={{12,0},{13,1},{14,2},{15,3},{28,16},{29,17},{30,18},{31,19},{44,32... | collective-permute-start | bytes 196616 | tf_op jit(solution)/shard_map/ppermute | solution.py:238
  71.8 2.7 %kept_tile.1 = (bf16[2,64,2048]{2,1,0:T(8,128)(2,1)}, bf16[2,64,2048]{2,1,0:T(8,128)(2,1)}, bf16[2,64,256]{2,1,0:T(8,128)(2,1)}, bf16[2,64,256]{2,1,0:T(8,128)(2,1)}) custom-call(s32[1,2]{1,0:T(1,128)S(1)} %copy-done.11, bf16[2,64,2048]{2,1,0:T(8,128)(2,1)S(1)} %bitcast.18, bf16[2,64,2048]{2,1,0:T(8,128)(2,1)S(1)} %bitcast.20, ...), custom_call_target="tpu_custom_call" | custom-call | flops 100663296 | bytes 1048576 | tf_op jit(solution)/shard_map/kept_tile/pallas_call | solution.py:208
  74.5 7.2 %collective-permute-done.6.refs_2_ = bf16[128,256]{1,0:T(8,128)(2,1)S(1)} collective-permute-done((bf16[128,256]{1,0:T(8,128)(2,1)S(1)}, bf16[128,256]{1,0:T(8,128)(2,1)S(1)}, u32[]{:S(2)}, u32[]{:S(2)}) %collective-permute-start.6) | collective-permute-done | bytes 65568 | tf_op jit(solution)/shard_map/ppermute | solution.py:238
  82.6 2.2 %moved_tile.1 = (bf16[2,64,2048]{2,1,0:T(8,128)(2,1)}, bf16[2,64,2048]{2,1,0:T(8,128)(2,1)}, bf16[2,64,256]{2,1,0:T(8,128)(2,1)}, bf16[2,64,256]{2,1,0:T(8,128)(2,1)}) custom-call(bf16[64,4736]{1,0:T(8,128)(2,1)S(1)} %collective-permute-done.11.early_ref, ...), custom_call_target="tpu_custom_call", output_to_operand_aliasing={{0}: (2, {}), {1}: (3, {}), {2}: (4, {}), {3}: (5, {})} | custom-call | flops 100663296 | bytes 1048576 | tf_op jit(solution)/shard_map/moved_tile/pallas_call | solution.py:242
  (37 shorter events, 4.2 us)
Async XLA Ops:
  1.3 1.0 %copy-start = (bf16[1,2,64,2048]{3,2,1,0:T(8,128)(2,1)S(1)}, bf16[1,2,64,2048]{3,2,1,0:T(8,128)(2,1)}, u32[]{:S(2)}) copy-start(bf16[1,2,64,2048]{3,2,1,0:T(8,128)(2,1)} %param.14) | copy-start | bytes 1572868
  2.4 1.0 %copy-start.2 = (bf16[1,2,64,2048]{3,2,1,0:T(8,128)(2,1)S(1)}, bf16[1,2,64,2048]{3,2,1,0:T(8,128)(2,1)}, u32[]{:S(2)}) copy-start(bf16[1,2,64,2048]{3,2,1,0:T(8,128)(2,1)} %param.17) | copy-start | bytes 1572868
  3.4 0.8 copy-start.6
  5.1 5.1 %copy-start.12 = (bf16[1,128,256]{2,1,0:T(8,128)(2,1)S(1)}, bf16[1,128,256]{2,1,0:T(8,128)(2,1)}, u32[]{:S(2)}) copy-start(bf16[1,128,256]{2,1,0:T(8,128)(2,1)} %param.12) | copy-start | bytes 196612
  5.1 5.1 %copy-start.13 = (bf16[1,128,256]{2,1,0:T(8,128)(2,1)S(1)}, bf16[1,128,256]{2,1,0:T(8,128)(2,1)}, u32[]{:S(2)}) copy-start(bf16[1,128,256]{2,1,0:T(8,128)(2,1)} %param.11) | copy-start | bytes 196612
  5.1 41.0 %copy-start.4 = (bf16[1,128,2048]{2,1,0:T(8,128)(2,1)S(1)}, bf16[1,128,2048]{2,1,0:T(8,128)(2,1)}, u32[]{:S(2)}) copy-start(bf16[1,128,2048]{2,1,0:T(8,128)(2,1)} %param.10) | copy-start | bytes 1572868
  5.1 41.0 %copy-start.5 = (bf16[1,128,2048]{2,1,0:T(8,128)(2,1)S(1)}, bf16[1,128,2048]{2,1,0:T(8,128)(2,1)}, u32[]{:S(2)}) copy-start(bf16[1,128,2048]{2,1,0:T(8,128)(2,1)} %param.13) | copy-start | bytes 1572868
  5.7 77.0 %collective-permute-start.12 = (bf16[64,4736]{1,0:T(8,128)(2,1)S(1)}, bf16[64,4736]{1,0:T(8,128)(2,1)S(1)}, u32[]{:S(2)}, u32[]{:S(2)}) collective-permute-start(bf16[64,4736]{1,0:T(8,128)(2,1)S(1)} %pack_tile.1), channel_id=1, source_target_pairs={{752,0},{753,1},{754,2},{755,3}} | collective-permute-start | bytes 1818632 | tf_op jit(solution)/shard_map/ppermute | solution.py:204
  6.4 76.2 %collective-permute-start.11 = (bf16[64,4736]{1,0:T(8,128)(2,1)S(1)}, bf16[64,4736]{1,0:T(8,128)(2,1)S(1)}, u32[]{:S(2)}, u32[]{:S(2)}) collective-permute-start(bf16[64,4736]{1,0:T(8,128)(2,1)S(1)} %pack_tile.1), channel_id=1, source_target_pairs={{0,16},{4,20},{8,24},{12,28},{16,32},{20,36},{24,40},{28,44},{32,4... | collective-permute-start | bytes 1818632 | tf_op jit(solution)/shard_map/ppermute | solution.py:203
  10.2 24.4 %collective-permute-start.4 = (bf16[128,512]{1,0:T(8,128)(2,1)S(1)}, bf16[128,512]{1,0:T(8,128)(2,1)S(1)}, u32[]{:S(2)}, u32[]{:S(2)}) collective-permute-start(bf16[128,512]{1,0:T(8,128)(2,1)S(1)} %pad_maximum_fusion.refs_2_), channel_id=1, source_target_pairs={{0,12},{1,13},{2,14},{3,15},{16,28},{17,29},{18,30},{19,31},{32,44... | collective-permute-start | bytes 393224 | tf_op jit(solution)/shard_map/ppermute | solution.py:181
  23.6 12.3 %collective-permute-start.3 = (bf16[128,512]{1,0:T(8,128)(2,1)S(1)}, bf16[128,512]{1,0:T(8,128)(2,1)S(1)}, u32[]{:S(2)}, u32[]{:S(2)}) collective-permute-start(bf16[128,512]{1,0:T(8,128)(2,1)S(1)} %pad_maximum_fusion.refs_2_), channel_id=1, source_target_pairs={{4,12},{5,13},{6,14},{7,15},{20,28},{21,29},{22,30},{23,31},{36,44... | collective-permute-start | bytes 393224 | tf_op jit(solution)/shard_map/ppermute | solution.py:181
  24.3 13.0 %collective-permute-start.2 = (bf16[128,512]{1,0:T(8,128)(2,1)S(1)}, bf16[128,512]{1,0:T(8,128)(2,1)S(1)}, u32[]{:S(2)}, u32[]{:S(2)}) collective-permute-start(bf16[128,512]{1,0:T(8,128)(2,1)S(1)} %pad_maximum_fusion.refs_2_), channel_id=1, source_target_pairs={{8,12},{9,13},{10,14},{11,15},{24,28},{25,29},{26,30},{27,31},{40,... | collective-permute-start | bytes 393224 | tf_op jit(solution)/shard_map/ppermute | solution.py:181
  34.7 4.5 %collective-permute-start.1 = (bf16[128,512]{1,0:T(8,128)(2,1)S(1)}, bf16[128,512]{1,0:T(8,128)(2,1)S(1)}, u32[]{:S(2)}, u32[]{:S(2)}) collective-permute-start(bf16[128,512]{1,0:T(8,128)(2,1)S(1)} %pad_maximum_fusion.refs_2_), channel_id=1, source_target_pairs={{0,8},{1,9},{2,10},{3,11},{16,24},{17,25},{18,26},{19,27},{32,40},... | collective-permute-start | bytes 393224 | tf_op jit(solution)/shard_map/ppermute | solution.py:180
  36.0 10.1 %collective-permute-start = (bf16[128,512]{1,0:T(8,128)(2,1)S(1)}, bf16[128,512]{1,0:T(8,128)(2,1)S(1)}, u32[]{:S(2)}, u32[]{:S(2)}) collective-permute-start(bf16[128,512]{1,0:T(8,128)(2,1)S(1)} %pad_maximum_fusion.refs_2_), channel_id=1, source_target_pairs={{0,4},{4,8},{1,5},{5,9},{2,6},{6,10},{3,7},{7,11},{16,20},{20,24},... | collective-permute-start | bytes 393224 | tf_op jit(solution)/shard_map/ppermute | solution.py:180
  48.6 23.2 %copy-start.1 = (bf16[1,2,64,2048]{3,2,1,0:T(8,128)(2,1)S(1)}, bf16[1,2,64,2048]{3,2,1,0:T(8,128)(2,1)}, u32[]{:S(2)}) copy-start(bf16[1,2,64,2048]{3,2,1,0:T(8,128)(2,1)} %param.14) | copy-start | bytes 1572868
  48.6 23.2 %copy-start.3 = (bf16[1,2,64,2048]{3,2,1,0:T(8,128)(2,1)S(1)}, bf16[1,2,64,2048]{3,2,1,0:T(8,128)(2,1)}, u32[]{:S(2)}) copy-start(bf16[1,2,64,2048]{3,2,1,0:T(8,128)(2,1)} %param.17) | copy-start | bytes 1572868
  48.6 23.2 %copy-start.7 = (bf16[1,2,64,256]{3,2,1,0:T(8,128)(2,1)S(1)}, bf16[1,2,64,256]{3,2,1,0:T(8,128)(2,1)}, u32[]{:S(2)}) copy-start(bf16[1,2,64,256]{3,2,1,0:T(8,128)(2,1)} %param.15) | copy-start | bytes 196612
  48.6 23.2 %copy-start.9 = (bf16[1,2,64,256]{3,2,1,0:T(8,128)(2,1)S(1)}, bf16[1,2,64,256]{3,2,1,0:T(8,128)(2,1)}, u32[]{:S(2)}) copy-start(bf16[1,2,64,256]{3,2,1,0:T(8,128)(2,1)} %param.16) | copy-start | bytes 196612
  51.2 12.0 %collective-permute-start.8 = (bf16[128,256]{1,0:T(8,128)(2,1)S(1)}, bf16[128,256]{1,0:T(8,128)(2,1)S(1)}, u32[]{:S(2)}, u32[]{:S(2)}) collective-permute-start(bf16[128,256]{1,0:T(8,128)(2,1)S(1)} %get-tuple-element.39), channel_id=1, source_target_pairs={{4,0},{8,4},{12,8},{5,1},{9,5},{13,9},{6,2},{10,6},{14,10},{7,3},{... | collective-permute-start | bytes 196616 | tf_op jit(solution)/shard_map/ppermute | solution.py:238
  52.5 16.7 %collective-permute-start.9 = (bf16[128,256]{1,0:T(8,128)(2,1)S(1)}, bf16[128,256]{1,0:T(8,128)(2,1)S(1)}, u32[]{:S(2)}, u32[]{:S(2)}) collective-permute-start(bf16[128,256]{1,0:T(8,128)(2,1)S(1)} %get-tuple-element.40), channel_id=1, source_target_pairs={{8,0},{12,4},{9,1},{13,5},{10,2},{14,6},{11,3},{15,7},{24,16},{28,... | collective-permute-start | bytes 196616 | tf_op jit(solution)/shard_map/ppermute | solution.py:238
  53.8 16.7 %collective-permute-start.10 = (bf16[128,256]{1,0:T(8,128)(2,1)S(1)}, bf16[128,256]{1,0:T(8,128)(2,1)S(1)}, u32[]{:S(2)}, u32[]{:S(2)}) collective-permute-start(bf16[128,256]{1,0:T(8,128)(2,1)S(1)} %get-tuple-element.41), channel_id=1, source_target_pairs={{12,0},{13,1},{14,2},{15,3},{28,16},{29,17},{30,18},{31,19},{44,32... | collective-permute-start | bytes 196616 | tf_op jit(solution)/shard_map/ppermute | solution.py:238
  63.1 11.4 %collective-permute-start.5 = (bf16[128,256]{1,0:T(8,128)(2,1)S(1)}, bf16[128,256]{1,0:T(8,128)(2,1)S(1)}, u32[]{:S(2)}, u32[]{:S(2)}) collective-permute-start(bf16[128,256]{1,0:T(8,128)(2,1)S(1)} %get-tuple-element.35), channel_id=1, source_target_pairs={{4,0},{8,4},{12,8},{5,1},{9,5},{13,9},{6,2},{10,6},{14,10},{7,3},{... | collective-permute-start | bytes 196616 | tf_op jit(solution)/shard_map/ppermute | solution.py:238
  69.2 12.6 %collective-permute-start.6 = (bf16[128,256]{1,0:T(8,128)(2,1)S(1)}, bf16[128,256]{1,0:T(8,128)(2,1)S(1)}, u32[]{:S(2)}, u32[]{:S(2)}) collective-permute-start(bf16[128,256]{1,0:T(8,128)(2,1)S(1)} %get-tuple-element.36), channel_id=1, source_target_pairs={{8,0},{12,4},{9,1},{13,5},{10,2},{14,6},{11,3},{15,7},{24,16},{28,... | collective-permute-start | bytes 196616 | tf_op jit(solution)/shard_map/ppermute | solution.py:238
  70.5 11.5 %collective-permute-start.7 = (bf16[128,256]{1,0:T(8,128)(2,1)S(1)}, bf16[128,256]{1,0:T(8,128)(2,1)S(1)}, u32[]{:S(2)}, u32[]{:S(2)}) collective-permute-start(bf16[128,256]{1,0:T(8,128)(2,1)S(1)} %get-tuple-element.37), channel_id=1, source_target_pairs={{12,0},{13,1},{14,2},{15,3},{28,16},{29,17},{30,18},{31,19},{44,32... | collective-permute-start | bytes 196616 | tf_op jit(solution)/shard_map/ppermute | solution.py:238
  (3 other events, 2.2 us)

commit v3 on v2

--- a/solution.py
+++ b/solution.py
@@ -81,8 +81,8 @@
     k_sum = jnp.zeros((HEAD, 4 * rows), F32)
     v_sum = jnp.zeros((HEAD, 4 * rows), F32)
     for first in range(0, 8, group):
-        q = heads_of(q_ref, first, group, slice(None))
-        g = heads_of(g_ref, first, group, slice(None))
+        q = heads_of(q_ref, head * 8 + first, group, slice(None))
+        g = heads_of(g_ref, head * 8 + first, group, slice(None))
         half, score_grad, out, q_grad = attend(q, g, k, v, bias)
         for j in range(group):
             at = slice((first + j) * HEAD, (first + j + 1) * HEAD)
@@ -147,6 +147,13 @@
         pack_ref.at[:, 0:2048], pack_ref.at[:, 2048:4096], pack_ref.at[:, 4096:4352],
         pack_ref.at[:, 4352:4608], labels, store,
     )
+
+
+def join(out_0, qg_0, out_1, qg_1, out_ref, qg_ref):
+    for h, (out, qg) in enumerate(((out_0, qg_0), (out_1, qg_1))):
+        at = slice(h * 8 * HEAD, (h + 1) * 8 * HEAD)
+        out_ref[:, at] = out[...]
+        qg_ref[:, at] = qg[...]
 
 
 def finish(*refs):
@@ -217,27 +224,27 @@
         cost_estimate=tile_cost, compiler_params=grant(16),
     )(assignment, *short, segments[0])
 
-    wide = [shaped(rows, 2048), shaped(rows, 2048)]
-    done = []
+    wide = []
     parts = []
     for h in range(2):
-        half_spec = pl.BlockSpec((rows, 1024), lambda i, h=h: (0, h))
         results = pl.pallas_call(
             lambda *refs, h=h: long_head(*refs, head=h, group=GROUP),
-            grid=(1,),
-            in_specs=[half_spec, half_spec] + [whole] * 6
-            + [pl.BlockSpec(memory_space=pl.ANY)] * len(done),
-            out_specs=[half_spec, half_spec] + [whole] * 4,
-            out_shape=wide + [shaped(rows, 256)] * 4,
-            input_output_aliases={8: 0, 9: 1} if done else {},
+            in_specs=[whole] * 8, out_specs=[whole] * 6,
+            out_shape=[shaped(rows, 1024)] * 2 + [shaped(rows, 256)] * 4,
             cost_estimate=cost(6 * 8 * 128 * 512 * 128, 3 << 19, 8 * 128 * 512),
             compiler_params=grant(24),
-        )(query_long[0], outgrad_long[0], packed, *near, *far, *done)
-        done = results[:2]
+        )(query_long[0], outgrad_long[0], packed, *near, *far)
+        wide += results[:2]
         parts += [results[2]] + [
             lax.ppermute(part, "ctx", [(c, c - step) for c in range(step, size)])
             for step, part in zip((1, 2, 3), results[3:])
         ]
+    done = pl.pallas_call(
+        join, grid=(1,), in_specs=[whole] * 4,
+        out_specs=[pl.BlockSpec((rows, 2048), lambda i: (0, 0))] * 2,
+        out_shape=[shaped(rows, 2048)] * 2, name="join",
+        cost_estimate=cost(0, 1 << 21, 0), compiler_params=grant(6),
+    )(*wide)
 
     tiles = pl.pallas_call(
         moved_kernel,

time: 85.4 us -> 82.5 us (0.966)
  the two profiles are of different devices: /device:TPU:77 before, /device:TPU:122 now
where the time goes in v3:
time: 82.5 us; the launch traced here: 81.9 us
  waiting for transfers between devices  37.3 us (45%)
  starting transfers between devices  28.1 us (34%)
  Pallas kernels  11.2 us (14%)
  local copies, waits for them, and re-layouts  4.47 us (5%)
  between operations  0.9 us (1%)
    ppermute x6, waiting for transfers between devices, work(): lax.ppermute(part, 'ctx', [(c, c - step) for c in range(step, size)])  17.6 us
    ppermute x3, starting transfers between devices, work(): lax.ppermute(packed, 'ctx', [(last - step, last)])  15 us
    ppermute x3, waiting for transfers between devices, work(): lax.ppermute(packed, 'ctx', [(last - step, last)])  10.8 us
    ppermute x2, waiting for transfers between devices, work(): lax.ppermute(packed, 'ctx', [(c, c + step) for c in range(last - step)])  8.87 us
    ppermute x6, starting transfers between devices, work(): lax.ppermute(part, 'ctx', [(c, c - step) for c in range(step, size)])  7.85 us
    unnamed x28, local copies, waits for them, and re-layouts  4.47 us
    pallas_call x2, Pallas kernels, work(): pl.pallas_call(lambda *refs, h=h: long_head(*refs, head=h, group=GROUP),...  3.95 us
    pallas_call x1, Pallas kernels, work(): pl.pallas_call(kept_kernel, grid_spec=pltpu.PrefetchScalarGridSpec(num_sc...  2.72 us
  transfers between devices with their start and end apart: 13, of which 8 were waited for; matrix products, arithmetic and copies ran while one was open for 0% of the time, Pallas kernels for 10%

profile of v3, /device:TPU:122, one launch (start us, length us, event | category | flops | bytes accessed | tf_op | source)
XLA Modules:
  0.0 81.9 jit_solution(12505939656298993724)
XLA Ops:
  1.3 1.0 %copy-done.2 = bf16[1,2,64,2048]{3,2,1,0:T(8,128)(2,1)S(1)} copy-done((bf16[1,2,64,2048]{3,2,1,0:T(8,128)(2,1)S(1)}, bf16[1,2,64,2048]{3,2,1,0:T(8,128)(2,1)}, u32[]{:S(2)}) %copy-start.2) | copy-done | bytes 524312
  2.4 1.0 %copy-done.4 = bf16[1,2,64,2048]{3,2,1,0:T(8,128)(2,1)S(1)} copy-done((bf16[1,2,64,2048]{3,2,1,0:T(8,128)(2,1)S(1)}, bf16[1,2,64,2048]{3,2,1,0:T(8,128)(2,1)}, u32[]{:S(2)}) %copy-start.4) | copy-done | bytes 524312
  6.4 1.9 %collective-permute-start.11 = (bf16[64,4736]{1,0:T(8,128)(2,1)S(1)}, bf16[64,4736]{1,0:T(8,128)(2,1)S(1)}, u32[]{:S(2)}, u32[]{:S(2)}) collective-permute-start(bf16[64,4736]{1,0:T(8,128)(2,1)S(1)} %pack_tile.1), channel_id=1, source_target_pairs={{0,16},{4,20},{8,24},{12,28},{16,32},{20,36},{24,40},{28,44},{32,4... | collective-permute-start | bytes 1818632 | tf_op jit(solution)/shard_map/ppermute | solution.py:210
  8.4 13.7 %collective-permute-start.4 = (bf16[128,512]{1,0:T(8,128)(2,1)S(1)}, bf16[128,512]{1,0:T(8,128)(2,1)S(1)}, u32[]{:S(2)}, u32[]{:S(2)}) collective-permute-start(bf16[128,512]{1,0:T(8,128)(2,1)S(1)} %pad_maximum_fusion.refs_2_), channel_id=1, source_target_pairs={{0,12},{1,13},{2,14},{3,15},{16,28},{17,29},{18,30},{19,31},{32,44... | collective-permute-start | bytes 393224 | tf_op jit(solution)/shard_map/ppermute | solution.py:188
  23.4 10.8 %collective-permute-done.4.refs_7_ = bf16[128,512]{1,0:T(8,128)(2,1)S(1)} collective-permute-done((bf16[128,512]{1,0:T(8,128)(2,1)S(1)}, bf16[128,512]{1,0:T(8,128)(2,1)S(1)}, u32[]{:S(2)}, u32[]{:S(2)}) %collective-permute-start.4) | collective-permute-done | bytes 131104 | tf_op jit(solution)/shard_map/ppermute | solution.py:188
  34.2 1.3 %collective-permute-start.1 = (bf16[128,512]{1,0:T(8,128)(2,1)S(1)}, bf16[128,512]{1,0:T(8,128)(2,1)S(1)}, u32[]{:S(2)}, u32[]{:S(2)}) collective-permute-start(bf16[128,512]{1,0:T(8,128)(2,1)S(1)} %pad_maximum_fusion.refs_2_), channel_id=1, source_target_pairs={{0,8},{1,9},{2,10},{3,11},{16,24},{17,25},{18,26},{19,27},{32,40},... | collective-permute-start | bytes 393224 | tf_op jit(solution)/shard_map/ppermute | solution.py:187
  35.5 1.3 %collective-permute-start = (bf16[128,512]{1,0:T(8,128)(2,1)S(1)}, bf16[128,512]{1,0:T(8,128)(2,1)S(1)}, u32[]{:S(2)}, u32[]{:S(2)}) collective-permute-start(bf16[128,512]{1,0:T(8,128)(2,1)S(1)} %pad_maximum_fusion.refs_2_), channel_id=1, source_target_pairs={{0,4},{4,8},{1,5},{5,9},{2,6},{6,10},{3,7},{7,11},{16,20},{20,24},... | collective-permute-start | bytes 393224 | tf_op jit(solution)/shard_map/ppermute | solution.py:187
  36.8 2.0 %collective-permute-done.1.refs_4_ = bf16[128,512]{1,0:T(8,128)(2,1)S(1)} collective-permute-done((bf16[128,512]{1,0:T(8,128)(2,1)S(1)}, bf16[128,512]{1,0:T(8,128)(2,1)S(1)}, u32[]{:S(2)}, u32[]{:S(2)}) %collective-permute-start.1) | collective-permute-done | bytes 131104 | tf_op jit(solution)/shard_map/ppermute | solution.py:187
  38.8 6.9 %collective-permute-done.refs_3_ = bf16[128,512]{1,0:T(8,128)(2,1)S(1)} collective-permute-done((bf16[128,512]{1,0:T(8,128)(2,1)S(1)}, bf16[128,512]{1,0:T(8,128)(2,1)S(1)}, u32[]{:S(2)}, u32[]{:S(2)}) %collective-permute-start) | collective-permute-done | bytes 131104 | tf_op jit(solution)/shard_map/ppermute | solution.py:187
  45.7 2.0 %shard_map.161 = (bf16[128,1024]{1,0:T(8,128)(2,1)S(1)}, bf16[128,1024]{1,0:T(8,128)(2,1)S(1)}, bf16[128,256]{1,0:T(8,128)(2,1)S(1)}, bf16[128,256]{1,0:T(8,128)...) custom-call(bf16[128,2048]{1,0:T(8,128)(2,1)S(1)} %bitcast.17, bf16[128,2048]{1,0:T(8,128)(2,1)S(1)} %bitcast.19, ...), custom_call_target="tpu_custom_call" | custom-call | flops 402653184 | bytes 1572864 | tf_op jit(solution)/shard_map/pallas_call | solution.py:230
  47.7 1.3 %collective-permute-start.5 = (bf16[128,256]{1,0:T(8,128)(2,1)S(1)}, bf16[128,256]{1,0:T(8,128)(2,1)S(1)}, u32[]{:S(2)}, u32[]{:S(2)}) collective-permute-start(bf16[128,256]{1,0:T(8,128)(2,1)S(1)} %get-tuple-element.39), channel_id=1, source_target_pairs={{4,0},{8,4},{12,8},{5,1},{9,5},{13,9},{6,2},{10,6},{14,10},{7,3},{... | collective-permute-start | bytes 196616 | tf_op jit(solution)/shard_map/ppermute | solution.py:239
  49.0 1.3 %collective-permute-start.6 = (bf16[128,256]{1,0:T(8,128)(2,1)S(1)}, bf16[128,256]{1,0:T(8,128)(2,1)S(1)}, u32[]{:S(2)}, u32[]{:S(2)}) collective-permute-start(bf16[128,256]{1,0:T(8,128)(2,1)S(1)} %get-tuple-element.40), channel_id=1, source_target_pairs={{8,0},{12,4},{9,1},{13,5},{10,2},{14,6},{11,3},{15,7},{24,16},{28,... | collective-permute-start | bytes 196616 | tf_op jit(solution)/shard_map/ppermute | solution.py:239
  50.3 1.4 %collective-permute-start.7 = (bf16[128,256]{1,0:T(8,128)(2,1)S(1)}, bf16[128,256]{1,0:T(8,128)(2,1)S(1)}, u32[]{:S(2)}, u32[]{:S(2)}) collective-permute-start(bf16[128,256]{1,0:T(8,128)(2,1)S(1)} %get-tuple-element.41), channel_id=1, source_target_pairs={{12,0},{13,1},{14,2},{15,3},{28,16},{29,17},{30,18},{31,19},{44,32... | collective-permute-start | bytes 196616 | tf_op jit(solution)/shard_map/ppermute | solution.py:239
  51.7 2.0 %shard_map.162 = (bf16[128,1024]{1,0:T(8,128)(2,1)S(1)}, bf16[128,1024]{1,0:T(8,128)(2,1)S(1)}, bf16[128,256]{1,0:T(8,128)(2,1)S(1)}, bf16[128,256]{1,0:T(8,128)...) custom-call(bf16[128,2048]{1,0:T(8,128)(2,1)S(1)} %bitcast.18, bf16[128,2048]{1,0:T(8,128)(2,1)S(1)} %bitcast.20, ...), custom_call_target="tpu_custom_call" | custom-call | flops 402653184 | bytes 1572864 | tf_op jit(solution)/shard_map/pallas_call | solution.py:230
  53.7 4.6 %collective-permute-done.5.refs_1_ = bf16[128,256]{1,0:T(8,128)(2,1)S(1)} collective-permute-done((bf16[128,256]{1,0:T(8,128)(2,1)S(1)}, bf16[128,256]{1,0:T(8,128)(2,1)S(1)}, u32[]{:S(2)}, u32[]{:S(2)}) %collective-permute-start.5) | collective-permute-done | bytes 65568 | tf_op jit(solution)/shard_map/ppermute | solution.py:239
  58.3 1.3 %collective-permute-start.8 = (bf16[128,256]{1,0:T(8,128)(2,1)S(1)}, bf16[128,256]{1,0:T(8,128)(2,1)S(1)}, u32[]{:S(2)}, u32[]{:S(2)}) collective-permute-start(bf16[128,256]{1,0:T(8,128)(2,1)S(1)} %get-tuple-element.43), channel_id=1, source_target_pairs={{4,0},{8,4},{12,8},{5,1},{9,5},{13,9},{6,2},{10,6},{14,10},{7,3},{... | collective-permute-start | bytes 196616 | tf_op jit(solution)/shard_map/ppermute | solution.py:239
  59.6 5.0 %collective-permute-done.6.refs_2_ = bf16[128,256]{1,0:T(8,128)(2,1)S(1)} collective-permute-done((bf16[128,256]{1,0:T(8,128)(2,1)S(1)}, bf16[128,256]{1,0:T(8,128)(2,1)S(1)}, u32[]{:S(2)}, u32[]{:S(2)}) %collective-permute-start.6) | collective-permute-done | bytes 65568 | tf_op jit(solution)/shard_map/ppermute | solution.py:239
  64.6 1.3 %collective-permute-start.9 = (bf16[128,256]{1,0:T(8,128)(2,1)S(1)}, bf16[128,256]{1,0:T(8,128)(2,1)S(1)}, u32[]{:S(2)}, u32[]{:S(2)}) collective-permute-start(bf16[128,256]{1,0:T(8,128)(2,1)S(1)} %get-tuple-element.44), channel_id=1, source_target_pairs={{8,0},{12,4},{9,1},{13,5},{10,2},{14,6},{11,3},{15,7},{24,16},{28,... | collective-permute-start | bytes 196616 | tf_op jit(solution)/shard_map/ppermute | solution.py:239
  66.5 1.3 %collective-permute-start.10 = (bf16[128,256]{1,0:T(8,128)(2,1)S(1)}, bf16[128,256]{1,0:T(8,128)(2,1)S(1)}, u32[]{:S(2)}, u32[]{:S(2)}) collective-permute-start(bf16[128,256]{1,0:T(8,128)(2,1)S(1)} %get-tuple-element.45), channel_id=1, source_target_pairs={{12,0},{13,1},{14,2},{15,3},{28,16},{29,17},{30,18},{31,19},{44,32... | collective-permute-start | bytes 196616 | tf_op jit(solution)/shard_map/ppermute | solution.py:239
  67.8 2.7 %kept_tile.1 = (bf16[2,64,2048]{2,1,0:T(8,128)(2,1)}, bf16[2,64,2048]{2,1,0:T(8,128)(2,1)}, bf16[2,64,256]{2,1,0:T(8,128)(2,1)}, bf16[2,64,256]{2,1,0:T(8,128)(2,1)}) custom-call(s32[1,2]{1,0:T(1,128)S(1)} %copy-done.11, bf16[2,64,2048]{2,1,0:T(8,128)(2,1)S(1)} %bitcast.22, bf16[2,64,2048]{2,1,0:T(8,128)(2,1)S(1)} %bitcast.24, ...), custom_call_target="tpu_custom_call" | custom-call | flops 100663296 | bytes 1048576 | tf_op jit(solution)/shard_map/kept_tile/pallas_call | solution.py:215
  70.5 1.0 %join.1 = (bf16[128,2048]{1,0:T(8,128)(2,1)}, bf16[128,2048]{1,0:T(8,128)(2,1)}) custom-call(bf16[128,1024]{1,0:T(8,128)(2,1)S(1)} %get-tuple-element.32.out_0, bf16[128,1024]{1,0:T(8,128)(2,1)S(1)} %get-tuple-element.33.qg_0, bf16[128,1024]{1,0:T(8,128)(2,1)S(1)} %get-tuple-element.34.out_1, bf16[128,1024]{1,0:T(8,128)(2,1)S(1)} %get-tuple-element.35.qg_1), custom_call_target="tpu_custom_call" | custom-call | bytes 2097152 | tf_op jit(solution)/shard_map/join/pallas_call | solution.py:242
  71.6 5.8 %collective-permute-done.9.refs_6_ = bf16[128,256]{1,0:T(8,128)(2,1)S(1)} collective-permute-done((bf16[128,256]{1,0:T(8,128)(2,1)S(1)}, bf16[128,256]{1,0:T(8,128)(2,1)S(1)}, u32[]{:S(2)}, u32[]{:S(2)}) %collective-permute-start.9) | collective-permute-done | bytes 65568 | tf_op jit(solution)/shard_map/ppermute | solution.py:239
  77.3 1.7 %collective-permute-done.10.refs_7_ = bf16[128,256]{1,0:T(8,128)(2,1)S(1)} collective-permute-done((bf16[128,256]{1,0:T(8,128)(2,1)S(1)}, bf16[128,256]{1,0:T(8,128)(2,1)S(1)}, u32[]{:S(2)}, u32[]{:S(2)}) %collective-permute-start.10) | collective-permute-done | bytes 65568 | tf_op jit(solution)/shard_map/ppermute | solution.py:239
  79.7 2.2 %moved_tile.1 = (bf16[2,64,2048]{2,1,0:T(8,128)(2,1)}, bf16[2,64,2048]{2,1,0:T(8,128)(2,1)}, bf16[2,64,256]{2,1,0:T(8,128)(2,1)}, bf16[2,64,256]{2,1,0:T(8,128)(2,1)}) custom-call(bf16[64,4736]{1,0:T(8,128)(2,1)S(1)} %collective-permute-done.11.early_ref, ...), custom_call_target="tpu_custom_call", output_to_operand_aliasing={{0}: (2, {}), {1}: (3, {}), {2}: (4, {}), {3}: (5, {})} | custom-call | flops 100663296 | bytes 1048576 | tf_op jit(solution)/shard_map/moved_tile/pallas_call | solution.py:249
  (38 shorter events, 6.3 us)
Async XLA Ops:
  1.3 1.0 %copy-start.2 = (bf16[1,2,64,2048]{3,2,1,0:T(8,128)(2,1)S(1)}, bf16[1,2,64,2048]{3,2,1,0:T(8,128)(2,1)}, u32[]{:S(2)}) copy-start(bf16[1,2,64,2048]{3,2,1,0:T(8,128)(2,1)} %param.14) | copy-start | bytes 1572868
  2.4 1.0 %copy-start.4 = (bf16[1,2,64,2048]{3,2,1,0:T(8,128)(2,1)S(1)}, bf16[1,2,64,2048]{3,2,1,0:T(8,128)(2,1)}, u32[]{:S(2)}) copy-start(bf16[1,2,64,2048]{3,2,1,0:T(8,128)(2,1)} %param.17) | copy-start | bytes 1572868
  3.4 0.8 %copy-start.6 = (bf16[1,2,64,256]{3,2,1,0:T(8,128)(2,1)S(1)}, bf16[1,2,64,256]{3,2,1,0:T(8,128)(2,1)}, u32[]{:S(2)}) copy-start(bf16[1,2,64,256]{3,2,1,0:T(8,128)(2,1)} %param.15) | copy-start | bytes 196612
  5.1 3.2 %copy-start.12 = (bf16[1,128,256]{2,1,0:T(8,128)(2,1)S(1)}, bf16[1,128,256]{2,1,0:T(8,128)(2,1)}, u32[]{:S(2)}) copy-start(bf16[1,128,256]{2,1,0:T(8,128)(2,1)} %param.12) | copy-start | bytes 196612
  5.1 3.3 %copy-start.13 = (bf16[1,128,256]{2,1,0:T(8,128)(2,1)S(1)}, bf16[1,128,256]{2,1,0:T(8,128)(2,1)}, u32[]{:S(2)}) copy-start(bf16[1,128,256]{2,1,0:T(8,128)(2,1)} %param.11) | copy-start | bytes 196612
  5.1 40.6 %copy-start = (bf16[1,128,2048]{2,1,0:T(8,128)(2,1)S(1)}, bf16[1,128,2048]{2,1,0:T(8,128)(2,1)}, u32[]{:S(2)}) copy-start(bf16[1,128,2048]{2,1,0:T(8,128)(2,1)} %param.10) | copy-start | bytes 1572868
  5.1 40.6 %copy-start.1 = (bf16[1,128,2048]{2,1,0:T(8,128)(2,1)S(1)}, bf16[1,128,2048]{2,1,0:T(8,128)(2,1)}, u32[]{:S(2)}) copy-start(bf16[1,128,2048]{2,1,0:T(8,128)(2,1)} %param.13) | copy-start | bytes 1572868
  5.7 74.0 %collective-permute-start.12 = (bf16[64,4736]{1,0:T(8,128)(2,1)S(1)}, bf16[64,4736]{1,0:T(8,128)(2,1)S(1)}, u32[]{:S(2)}, u32[]{:S(2)}) collective-permute-start(bf16[64,4736]{1,0:T(8,128)(2,1)S(1)} %pack_tile.1), channel_id=1, source_target_pairs={{752,0},{753,1},{754,2},{755,3}} | collective-permute-start | bytes 1818632 | tf_op jit(solution)/shard_map/ppermute | solution.py:211
  6.4 73.3 %collective-permute-start.11 = (bf16[64,4736]{1,0:T(8,128)(2,1)S(1)}, bf16[64,4736]{1,0:T(8,128)(2,1)S(1)}, u32[]{:S(2)}, u32[]{:S(2)}) collective-permute-start(bf16[64,4736]{1,0:T(8,128)(2,1)S(1)} %pack_tile.1), channel_id=1, source_target_pairs={{0,16},{4,20},{8,24},{12,28},{16,32},{20,36},{24,40},{28,44},{32,4... | collective-permute-start | bytes 1818632 | tf_op jit(solution)/shard_map/ppermute | solution.py:210
  8.4 25.8 %collective-permute-start.4 = (bf16[128,512]{1,0:T(8,128)(2,1)S(1)}, bf16[128,512]{1,0:T(8,128)(2,1)S(1)}, u32[]{:S(2)}, u32[]{:S(2)}) collective-permute-start(bf16[128,512]{1,0:T(8,128)(2,1)S(1)} %pad_maximum_fusion.refs_2_), channel_id=1, source_target_pairs={{0,12},{1,13},{2,14},{3,15},{16,28},{17,29},{18,30},{19,31},{32,44... | collective-permute-start | bytes 393224 | tf_op jit(solution)/shard_map/ppermute | solution.py:188
  22.0 13.4 %collective-permute-start.3 = (bf16[128,512]{1,0:T(8,128)(2,1)S(1)}, bf16[128,512]{1,0:T(8,128)(2,1)S(1)}, u32[]{:S(2)}, u32[]{:S(2)}) collective-permute-start(bf16[128,512]{1,0:T(8,128)(2,1)S(1)} %pad_maximum_fusion.refs_2_), channel_id=1, source_target_pairs={{4,12},{5,13},{6,14},{7,15},{20,28},{21,29},{22,30},{23,31},{36,44... | collective-permute-start | bytes 393224 | tf_op jit(solution)/shard_map/ppermute | solution.py:188
  22.7 14.1 %collective-permute-start.2 = (bf16[128,512]{1,0:T(8,128)(2,1)S(1)}, bf16[128,512]{1,0:T(8,128)(2,1)S(1)}, u32[]{:S(2)}, u32[]{:S(2)}) collective-permute-start(bf16[128,512]{1,0:T(8,128)(2,1)S(1)} %pad_maximum_fusion.refs_2_), channel_id=1, source_target_pairs={{8,12},{9,13},{10,14},{11,15},{24,28},{25,29},{26,30},{27,31},{40,... | collective-permute-start | bytes 393224 | tf_op jit(solution)/shard_map/ppermute | solution.py:188
  34.2 4.6 %collective-permute-start.1 = (bf16[128,512]{1,0:T(8,128)(2,1)S(1)}, bf16[128,512]{1,0:T(8,128)(2,1)S(1)}, u32[]{:S(2)}, u32[]{:S(2)}) collective-permute-start(bf16[128,512]{1,0:T(8,128)(2,1)S(1)} %pad_maximum_fusion.refs_2_), channel_id=1, source_target_pairs={{0,8},{1,9},{2,10},{3,11},{16,24},{17,25},{18,26},{19,27},{32,40},... | collective-permute-start | bytes 393224 | tf_op jit(solution)/shard_map/ppermute | solution.py:187
  35.5 10.2 %collective-permute-start = (bf16[128,512]{1,0:T(8,128)(2,1)S(1)}, bf16[128,512]{1,0:T(8,128)(2,1)S(1)}, u32[]{:S(2)}, u32[]{:S(2)}) collective-permute-start(bf16[128,512]{1,0:T(8,128)(2,1)S(1)} %pad_maximum_fusion.refs_2_), channel_id=1, source_target_pairs={{0,4},{4,8},{1,5},{5,9},{2,6},{6,10},{3,7},{7,11},{16,20},{20,24},... | collective-permute-start | bytes 393224 | tf_op jit(solution)/shard_map/ppermute | solution.py:187
  47.7 10.6 %collective-permute-start.5 = (bf16[128,256]{1,0:T(8,128)(2,1)S(1)}, bf16[128,256]{1,0:T(8,128)(2,1)S(1)}, u32[]{:S(2)}, u32[]{:S(2)}) collective-permute-start(bf16[128,256]{1,0:T(8,128)(2,1)S(1)} %get-tuple-element.39), channel_id=1, source_target_pairs={{4,0},{8,4},{12,8},{5,1},{9,5},{13,9},{6,2},{10,6},{14,10},{7,3},{... | collective-permute-start | bytes 196616 | tf_op jit(solution)/shard_map/ppermute | solution.py:239
  49.0 15.6 %collective-permute-start.6 = (bf16[128,256]{1,0:T(8,128)(2,1)S(1)}, bf16[128,256]{1,0:T(8,128)(2,1)S(1)}, u32[]{:S(2)}, u32[]{:S(2)}) collective-permute-start(bf16[128,256]{1,0:T(8,128)(2,1)S(1)} %get-tuple-element.40), channel_id=1, source_target_pairs={{8,0},{12,4},{9,1},{13,5},{10,2},{14,6},{11,3},{15,7},{24,16},{28,... | collective-permute-start | bytes 196616 | tf_op jit(solution)/shard_map/ppermute | solution.py:239
  50.3 17.5 %copy-start.3 = (bf16[1,2,64,2048]{3,2,1,0:T(8,128)(2,1)S(1)}, bf16[1,2,64,2048]{3,2,1,0:T(8,128)(2,1)}, u32[]{:S(2)}) copy-start(bf16[1,2,64,2048]{3,2,1,0:T(8,128)(2,1)} %param.14) | copy-start | bytes 1572868
  50.3 17.5 %copy-start.5 = (bf16[1,2,64,2048]{3,2,1,0:T(8,128)(2,1)S(1)}, bf16[1,2,64,2048]{3,2,1,0:T(8,128)(2,1)}, u32[]{:S(2)}) copy-start(bf16[1,2,64,2048]{3,2,1,0:T(8,128)(2,1)} %param.17) | copy-start | bytes 1572868
  50.3 17.5 %copy-start.7 = (bf16[1,2,64,256]{3,2,1,0:T(8,128)(2,1)S(1)}, bf16[1,2,64,256]{3,2,1,0:T(8,128)(2,1)}, u32[]{:S(2)}) copy-start(bf16[1,2,64,256]{3,2,1,0:T(8,128)(2,1)} %param.15) | copy-start | bytes 196612
  50.3 17.5 %copy-start.9 = (bf16[1,2,64,256]{3,2,1,0:T(8,128)(2,1)S(1)}, bf16[1,2,64,256]{3,2,1,0:T(8,128)(2,1)}, u32[]{:S(2)}) copy-start(bf16[1,2,64,256]{3,2,1,0:T(8,128)(2,1)} %param.16) | copy-start | bytes 196612
  50.3 16.2 %collective-permute-start.7 = (bf16[128,256]{1,0:T(8,128)(2,1)S(1)}, bf16[128,256]{1,0:T(8,128)(2,1)S(1)}, u32[]{:S(2)}, u32[]{:S(2)}) collective-permute-start(bf16[128,256]{1,0:T(8,128)(2,1)S(1)} %get-tuple-element.41), channel_id=1, source_target_pairs={{12,0},{13,1},{14,2},{15,3},{28,16},{29,17},{30,18},{31,19},{44,32... | collective-permute-start | bytes 196616 | tf_op jit(solution)/shard_map/ppermute | solution.py:239
  58.3 13.3 %collective-permute-start.8 = (bf16[128,256]{1,0:T(8,128)(2,1)S(1)}, bf16[128,256]{1,0:T(8,128)(2,1)S(1)}, u32[]{:S(2)}, u32[]{:S(2)}) collective-permute-start(bf16[128,256]{1,0:T(8,128)(2,1)S(1)} %get-tuple-element.43), channel_id=1, source_target_pairs={{4,0},{8,4},{12,8},{5,1},{9,5},{13,9},{6,2},{10,6},{14,10},{7,3},{... | collective-permute-start | bytes 196616 | tf_op jit(solution)/shard_map/ppermute | solution.py:239
  64.6 12.7 %collective-permute-start.9 = (bf16[128,256]{1,0:T(8,128)(2,1)S(1)}, bf16[128,256]{1,0:T(8,128)(2,1)S(1)}, u32[]{:S(2)}, u32[]{:S(2)}) collective-permute-start(bf16[128,256]{1,0:T(8,128)(2,1)S(1)} %get-tuple-element.44), channel_id=1, source_target_pairs={{8,0},{12,4},{9,1},{13,5},{10,2},{14,6},{11,3},{15,7},{24,16},{28,... | collective-permute-start | bytes 196616 | tf_op jit(solution)/shard_map/ppermute | solution.py:239
  66.5 12.6 %collective-permute-start.10 = (bf16[128,256]{1,0:T(8,128)(2,1)S(1)}, bf16[128,256]{1,0:T(8,128)(2,1)S(1)}, u32[]{:S(2)}, u32[]{:S(2)}) collective-permute-start(bf16[128,256]{1,0:T(8,128)(2,1)S(1)} %get-tuple-element.45), channel_id=1, source_target_pairs={{12,0},{13,1},{14,2},{15,3},{28,16},{29,17},{30,18},{31,19},{44,32... | collective-permute-start | bytes 196616 | tf_op jit(solution)/shard_map/ppermute | solution.py:239
  (3 other events, 2.2 us)
